TPU v7x, 256 devices: a whole 4x4x8 slice. The times are simulated.
256 devices in a mesh: req: 64 (over x_lo, y, z), ctx: 4 (over x_hi, core).
Axes of the slice: x: 4 (x_hi: 2, x_lo: 2; x = x_hi * 2 + x_lo), y: 4, z: 8, core: 2. Of those that a mesh axis runs over, the one named last changes fastest.
Arguments:
- q_nope: bfloat16 [64, 128, 8192], P('req'), may hold values from -6 to 6
- q_rope: bfloat16 [64, 128, 4096], P('req'), may hold values from -600 to 600
- cache_latent: bfloat16 [64, 1024, 512], P('req', 'ctx'), may hold values from -6 to 6
- cache_rope: bfloat16 [64, 1024, 64], P('req', 'ctx'), may hold values from -4 to 4
- new_latent: bfloat16 [64, 128, 512], P('req', 'ctx'), may hold values from -6 to 6
- new_rope: bfloat16 [64, 128, 64], P('req', 'ctx'), may hold values from -8 to 8
- lengths: int32 [64, 4], P('req', 'ctx'), may hold values from 64 to 256, as said below
- w_key: bfloat16 [512, 8192], P(None, 'ctx'), may hold values from -0.25 to 0.25
- w_value: bfloat16 [512, 8192], P(None, 'ctx'), may hold values from -0.25 to 0.25
Outputs:
- attended: bfloat16 [64, 128, 8192], P('req', None, 'ctx')
Inputs may be any that keep to these rules, and one draw needn't show every extreme that they name: lengths[r, g] counts the live cached rows at the start of request r's slots in context group g; all cached rows precede the new tokens; some entry equals 256 in every draw.
All inputs are finite; a program needn't handle non-finite values.
Results may differ from a plain program's by a relative error of at most 0.015.
Values may be sent and summed in bfloat16 or wider, within the bound.
A program may use at most 128 MiB of HBM per device.

v0:
```python
import math

import jax
import jax.numpy as jnp
from jax import lax
from jax.sharding import PartitionSpec as P

DR = 64
DH = 128
DV = 128
HEADS = 64
GROUP = 4
BLOCK = 256


blocked_score = -1e30


def expand_block(
    lat_rows, rope_keys, visible, query_nope, query_rope, weight_key, weight_value, running
):
    running_max, running_sum, running_out = running
    row_count = lat_rows.shape[0]
    score_scale = 1.0 / math.sqrt(DH + DR)
    key_rows = jnp.dot(lat_rows, weight_key, preferred_element_type=jnp.float32).astype(
        jnp.bfloat16
    )
    value_rows = jnp.dot(lat_rows, weight_value, preferred_element_type=jnp.float32).astype(
        jnp.bfloat16
    )
    key_rows = key_rows.reshape(row_count, GROUP, DH)
    value_rows = value_rows.reshape(row_count, GROUP, DV)
    scores = jnp.einsum("qhd,khd->qhk", query_nope, key_rows, preferred_element_type=jnp.float32)
    scores = scores + jnp.einsum(
        "qhd,kd->qhk", query_rope, rope_keys, preferred_element_type=jnp.float32
    )
    scores = jnp.where(visible[:, None, :], scores * score_scale, blocked_score)
    new_max = jnp.maximum(running_max, jnp.max(scores, axis=-1))
    factor = jnp.exp(running_max - new_max)
    weights = jnp.where(visible[:, None, :], jnp.exp(scores - new_max[..., None]), 0.0)
    running_sum = running_sum * factor + jnp.sum(weights, axis=-1)
    running_out = running_out * factor[..., None] + jnp.einsum(
        "qhk,khd->qhd", weights.astype(jnp.bfloat16), value_rows, preferred_element_type=jnp.float32
    )
    return (new_max, running_sum, running_out)


def start_running(query_count):
    return (
        jnp.full((query_count, GROUP), blocked_score, jnp.float32),
        jnp.zeros((query_count, GROUP), jnp.float32),
        jnp.zeros((query_count, GROUP, DV), jnp.float32),
    )


def cached_pass(
    running, query_nope, query_rope, weight_key, weight_value, cache_rows, cache_keys, live_rows
):

    def advance(block_index, running):
        offset = block_index * BLOCK
        visible = (offset + jnp.arange(BLOCK, dtype=jnp.int32))[None, :] < live_rows
        visible = jnp.broadcast_to(visible, (query_nope.shape[0], BLOCK))
        return expand_block(
            cache_rows,
            cache_keys,
            visible,
            query_nope,
            query_rope,
            weight_key,
            weight_value,
            running,
        )

    block_count = (live_rows + BLOCK - 1) // BLOCK
    return lax.fori_loop(0, block_count, advance, running)


def fresh_pass(
    running, query_nope, query_rope, weight_key, weight_value, fresh_rows, fresh_keys, fresh_first
):
    query_count = query_nope.shape[0]
    fresh_index = fresh_first + jnp.arange(fresh_rows.shape[0], dtype=jnp.int32)
    visible = fresh_index[None, :] <= jnp.arange(query_count, dtype=jnp.int32)[:, None]
    return expand_block(
        fresh_rows, fresh_keys, visible, query_nope, query_rope, weight_key, weight_value, running
    )


def shards(q_nope, q_rope, cache_latent, cache_rope, new_latent, new_rope, lengths, w_key, w_value):
    ctx_count = lax.axis_size("ctx")
    ctx_index = lax.axis_index("ctx")
    queries = q_nope[0]
    rotary = q_rope[0]
    query_count = queries.shape[0]
    width_key = GROUP * DH
    width_value = GROUP * DV
    heads_here = HEADS // ctx_count
    groups = HEADS // GROUP
    fresh_rows = new_latent[0]
    fresh_first = ctx_index * fresh_rows.shape[0]
    live_rows = lengths[0, 0]
    full_key, full_value = (
        lax.all_gather(w_key, "ctx", axis=1, tiled=True),
        lax.all_gather(w_value, "ctx", axis=1, tiled=True),
    )
    maxima = []
    sums = []
    outputs = []
    for group_index in range(groups):
        weight_key = full_key[:, group_index * width_key : (group_index + 1) * width_key]
        weight_value = full_value[:, group_index * width_value : (group_index + 1) * width_value]
        query_nope = queries[:, group_index * GROUP * DH : (group_index + 1) * GROUP * DH].reshape(
            query_count, GROUP, DH
        )
        query_rope = rotary[:, group_index * GROUP * DR : (group_index + 1) * GROUP * DR].reshape(
            query_count, GROUP, DR
        )
        running = start_running(query_count)
        running = cached_pass(
            running,
            query_nope,
            query_rope,
            weight_key,
            weight_value,
            cache_latent[0],
            cache_rope[0],
            live_rows,
        )
        group_max, group_sum, group_out = fresh_pass(
            running,
            query_nope,
            query_rope,
            weight_key,
            weight_value,
            fresh_rows,
            new_rope[0],
            fresh_first,
        )
        maxima.append(group_max)
        sums.append(group_sum)
        outputs.append(group_out)
    running_max = jnp.concatenate(maxima, axis=1)
    running_sum = jnp.concatenate(sums, axis=1)
    running_out = jnp.concatenate(outputs, axis=1)
    overall_max = lax.pmax(running_max.astype(jnp.bfloat16), "ctx").astype(running_max.dtype)
    factor = jnp.exp(running_max - overall_max)
    numerator, denominator = (
        lax.psum_scatter(
            (running_out * factor[..., None]).reshape(query_count, HEADS * DV).astype(jnp.bfloat16),
            "ctx",
            scatter_dimension=1,
            tiled=True,
        ).astype(jnp.float32),
        lax.psum_scatter(
            (running_sum * factor).astype(jnp.bfloat16), "ctx", scatter_dimension=1, tiled=True
        ).astype(jnp.float32),
    )
    numerator = numerator.reshape(query_count, heads_here, DV)
    attended = (numerator / denominator[..., None]).reshape(query_count, heads_here * DV)
    return attended.astype(jnp.bfloat16)[None]


def solution(mesh):
    return jax.shard_map(
        shards,
        mesh=mesh,
        in_specs=(
            P("req", None, None),
            P("req", None, None),
            P("req", "ctx", None),
            P("req", "ctx", None),
            P("req", "ctx", None),
            P("req", "ctx", None),
            P("req", "ctx"),
            P(None, "ctx"),
            P(None, "ctx"),
        ),
        out_specs=P("req", None, "ctx"),
        check_vma=False,
    )
```

profile of v0, /device:TPU:1, one launch (start us, length us, event | category | flops | bytes accessed | tf_op | source)
XLA Modules:
  0.0 420.9 jit_solution(1115684594973445940)
XLA Ops:
  8.7 1.3 fusion.675
  18.6 3.2 copy.204
  34.6 43.7 %all-gather.3.cloned.1.call-done = bf16[512,8192]{1,0:T(8,128)(2,1)} async-done(((bf16[512,2048]{1,0:T(8,128)(2,1)}), bf16[512,8192]{1,0:T(8,128)(2,1)}) %all-gather.3.cloned.1.call-update) | async-done | bytes 8388624 | tf_op jit(solution)/shard_map/all_gather | solution.py:104
  79.5 1.7 convolution_bitcast_fusion.48
  81.1 1.3 convolution_convert_fusion.1
  82.5 61.9 %all-gather.5.cloned.1.call-done = bf16[512,8192]{1,0:T(8,128)(2,1)} async-done(((bf16[512,2048]{1,0:T(8,128)(2,1)}), bf16[512,8192]{1,0:T(8,128)(2,1)}) %all-gather.5.cloned.1.call-update) | async-done | bytes 8388624 | tf_op jit(solution)/shard_map/all_gather | solution.py:105
  144.4 1.3 convolution_convert_fusion
  146.4 3.9 while.271
  152.3 1.7 convolution_bitcast_fusion.50
  154.0 1.3 convolution_convert_fusion.4
  155.3 1.3 convolution_convert_fusion.5
  157.9 5.1 %while.269 = (s32[]{:T(128)}, f32[128,4]{0,1:T(4,128)}, f32[128,4]{0,1:T(4,128)}, f32[128,4,128]{2,0,1:T(8,128)S(1)}, s32[]{:T(128)}, /*index=5*/s32[]{:T(128)},...) while((s32[]{:T(128)}, f32[128,4]{0,1:T(4,128)}, ...), condition=%wide.region_68.69_spmd, body=%wide.region_65.68_spmd.sunk | while | flops 85329408 | bytes 3933329 | solution.py:76
  163.9 2.2 fusion.676
  166.0 1.6 fusion.691
  168.8 1.7 convolution_bitcast_fusion.49
  171.9 1.3 convolution_convert_fusion.3
  173.3 1.8 while.270
  176.0 2.2 fusion.685
  179.4 1.7 convolution_bitcast_fusion.51
  182.4 1.3 convolution_convert_fusion.7
  183.8 1.8 while.268
  186.5 2.2 fusion.690
  190.7 1.3 convolution_convert_fusion.8
  192.1 1.3 convolution_convert_fusion.9
  193.5 1.9 while.267
  196.3 1.3 fusion.689
  199.7 1.3 convolution_convert_fusion.10
  201.0 1.3 convolution_convert_fusion.11
  202.4 2.0 while.266
  204.6 2.2 fusion.688
  208.8 1.3 convolution_convert_fusion.12
  210.2 1.3 convolution_convert_fusion.13
  211.6 1.9 while.265
  219.1 1.3 convolution_convert_fusion.15
  220.5 1.8 while.264
  222.5 2.2 fusion.686
  228.1 1.3 convolution_convert_fusion.17
  229.5 1.9 while.263
  232.2 1.3 fusion.684
  237.0 1.3 convolution_convert_fusion.19
  238.4 1.8 while.262
  240.4 2.2 fusion.683
  244.0 1.3 convolution_convert_fusion.20
  245.3 1.3 convolution_convert_fusion.21
  246.7 1.8 while.261
  252.2 1.3 convolution_convert_fusion.22
  253.5 1.3 convolution_convert_fusion.23
  254.9 1.8 while.260
  260.3 1.3 convolution_convert_fusion.24
  261.7 1.3 convolution_convert_fusion.25
  263.1 1.8 while.259
  268.5 1.3 convolution_convert_fusion.26
  269.9 1.3 convolution_convert_fusion.27
  271.3 2.0 while.258
  276.9 1.3 convolution_convert_fusion.28
  278.3 1.3 convolution_convert_fusion.29
  279.7 1.8 while.257
  287.1 1.3 convolution_convert_fusion.31
  288.5 1.8 while.256
  303.2 12.5 %pmax.7 = bf16[128,64]{0,1:T(8,128)(2,1)S(1)} all-reduce(bf16[128,64]{0,1:T(8,128)(2,1)S(1)} %convert_element_type.488), channel_id=1, replica_groups=mesh['req'=64,'ctx'=4] {'ctx'}, use_global_device_ids=true, to_apply=%region_80.81 | all-reduce | flops 8192 | bytes 32768 | tf_op jit(solution)/shard_map/pmax | solution.py:146
  327.0 1.3 multiply_add_fusion.25
  363.8 3.0 copy.301
  367.6 44.2 %reduce-scatter.3.cloned.1.call-done = bf16[128,2048]{1,0:T(8,128)(2,1)} async-done(((bf16[128,8192]{1,0:T(8,128)(2,1)}), bf16[128,2048]{1,0:T(8,128)(2,1)}) %reduce-scatter.3.cloned.1.call-update) | async-done | bytes 524304 | tf_op jit(solution)/shard_map/reduce_scatter | solution.py:149
  412.2 2.2 fusion.337
  (543 shorter events, 171.1 us)
Async XLA Ops:
  6.5 74.6 %copy-start = (bf16[1,256,512]{2,1,0:T(8,128)(2,1)S(1)}, bf16[1,256,512]{2,1,0:T(8,128)(2,1)}, u32[]{:S(2)}) copy-start(bf16[1,256,512]{2,1,0:T(8,128)(2,1)} %param.43) | copy-start | bytes 786436
  6.5 71.7 %all-gather.3.cloned.1.call-start = ((), (), s32[]{:S(2)}) async-start(), calls=%async_computation.2 | async-start | bytes 10485760 | tf_op jit(solution)/shard_map/all_gather | solution.py:104
  7.3 137.1 %all-gather.5.cloned.1.call-start = ((), (), s32[]{:S(2)}) async-start(), calls=%async_computation.3 | async-start | bytes 10485760 | tf_op jit(solution)/shard_map/all_gather | solution.py:105
  8.0 358.8 %reduce-scatter.5.cloned.1.call-start = ((), (), s32[]{:S(2)}) async-start(), calls=%async_computation.5 | async-start | bytes 20480 | tf_op jit(solution)/shard_map/reduce_scatter | solution.py:155
  8.7 69.5 %copy-start.2 = (bf16[1,32,512]{2,1,0:T(8,128)(2,1)S(1)}, bf16[1,32,512]{2,1,0:T(8,128)(2,1)}, u32[]{:S(2)}) copy-start(bf16[1,32,512]{2,1,0:T(8,128)(2,1)} %param.45) | copy-start | bytes 98308
  17.3 129.1 %copy-start.1 = (bf16[1,256,64]{1,2,0:T(8,128)(2,1)S(1)}, bf16[1,256,64]{1,2,0:T(8,128)(2,1)}, u32[]{:S(2)}) copy-start(bf16[1,256,64]{1,2,0:T(8,128)(2,1)} %param.44) | copy-start | bytes 98308
  22.9 10.8 %copy-start.24 = (bf16[128,512]{0,1:T(8,128)(2,1)}, bf16[128,512]{0,1:T(8,128)(2,1)S(1)}, u32[]{:S(2)}) copy-start(bf16[128,512]{0,1:T(8,128)(2,1)S(1)} %get-tuple-element.3009) | copy-start | bytes 393220
  22.9 11.0 %copy-start.22 = (bf16[128,512]{0,1:T(8,128)(2,1)}, bf16[128,512]{0,1:T(8,128)(2,1)S(1)}, u32[]{:S(2)}) copy-start(bf16[128,512]{0,1:T(8,128)(2,1)S(1)} %get-tuple-element.3010) | copy-start | bytes 393220
  22.9 11.1 %copy-start.20 = (bf16[128,512]{0,1:T(8,128)(2,1)}, bf16[128,512]{0,1:T(8,128)(2,1)S(1)}, u32[]{:S(2)}) copy-start(bf16[128,512]{0,1:T(8,128)(2,1)S(1)} %get-tuple-element.3011) | copy-start | bytes 393220
  22.9 11.2 %copy-start.18 = (bf16[128,512]{0,1:T(8,128)(2,1)}, bf16[128,512]{0,1:T(8,128)(2,1)S(1)}, u32[]{:S(2)}) copy-start(bf16[128,512]{0,1:T(8,128)(2,1)S(1)} %get-tuple-element.3012) | copy-start | bytes 393220
  22.9 11.4 %copy-start.16 = (bf16[128,512]{0,1:T(8,128)(2,1)}, bf16[128,512]{0,1:T(8,128)(2,1)S(1)}, u32[]{:S(2)}) copy-start(bf16[128,512]{0,1:T(8,128)(2,1)S(1)} %get-tuple-element.3013) | copy-start | bytes 393220
  22.9 122.8 %copy-start.14 = (bf16[128,512]{0,1:T(8,128)(2,1)}, bf16[128,512]{0,1:T(8,128)(2,1)S(1)}, u32[]{:S(2)}) copy-start(bf16[128,512]{0,1:T(8,128)(2,1)S(1)} %get-tuple-element.3014) | copy-start | bytes 393220
  157.8 6.0 %copy-start.12 = (bf16[128,4,64]{0,2,1:T(8,128)(2,1)S(1)}, bf16[128,4,64]{0,2,1:T(8,128)(2,1)}, u32[]{:S(2)}) copy-start(bf16[128,4,64]{0,2,1:T(8,128)(2,1)} %get-tuple-element.4957) | copy-start | bytes 196612
  157.9 15.4 %copy-start.11 = (bf16[128,256]{0,1:T(8,128)(2,1)S(1)}, bf16[128,256]{0,1:T(8,128)(2,1)}, u32[]{:S(2)}) copy-start(bf16[128,256]{0,1:T(8,128)(2,1)} %copy.289) | copy-start | bytes 196612
  173.3 10.5 %copy-start.10 = (bf16[128,256]{0,1:T(8,128)(2,1)S(1)}, bf16[128,256]{0,1:T(8,128)(2,1)}, u32[]{:S(2)}) copy-start(bf16[128,256]{0,1:T(8,128)(2,1)} %copy.277) | copy-start | bytes 196612
  183.8 6.1 %copy-start.31 = (bf16[128,512]{0,1:T(8,128)(2,1)S(1)}, bf16[128,512]{0,1:T(8,128)(2,1)}, u32[]{:S(2)}) copy-start(bf16[128,512]{0,1:T(8,128)(2,1)} %get-tuple-element.3003) | copy-start | bytes 393220
  183.8 9.7 %copy-start.9 = (bf16[128,256]{0,1:T(8,128)(2,1)S(1)}, bf16[128,256]{0,1:T(8,128)(2,1)}, u32[]{:S(2)}) copy-start(bf16[128,256]{0,1:T(8,128)(2,1)} %copy.271) | copy-start | bytes 196612
  193.5 8.9 %copy-start.8 = (bf16[128,256]{0,1:T(8,128)(2,1)S(1)}, bf16[128,256]{0,1:T(8,128)(2,1)}, u32[]{:S(2)}) copy-start(bf16[128,256]{0,1:T(8,128)(2,1)} %copy.265) | copy-start | bytes 196612
  202.4 9.2 %copy-start.7 = (bf16[128,256]{0,1:T(8,128)(2,1)S(1)}, bf16[128,256]{0,1:T(8,128)(2,1)}, u32[]{:S(2)}) copy-start(bf16[128,256]{0,1:T(8,128)(2,1)} %copy.259) | copy-start | bytes 196612
  211.6 8.9 %copy-start.6 = (bf16[128,256]{0,1:T(8,128)(2,1)S(1)}, bf16[128,256]{0,1:T(8,128)(2,1)}, u32[]{:S(2)}) copy-start(bf16[128,256]{0,1:T(8,128)(2,1)} %copy.253) | copy-start | bytes 196612
  220.5 9.0 %copy-start.5 = (bf16[128,256]{0,1:T(8,128)(2,1)S(1)}, bf16[128,256]{0,1:T(8,128)(2,1)}, u32[]{:S(2)}) copy-start(bf16[128,256]{0,1:T(8,128)(2,1)} %copy.247) | copy-start | bytes 196612
  229.5 8.9 %copy-start.4 = (bf16[128,256]{0,1:T(8,128)(2,1)S(1)}, bf16[128,256]{0,1:T(8,128)(2,1)}, u32[]{:S(2)}) copy-start(bf16[128,256]{0,1:T(8,128)(2,1)} %copy.241) | copy-start | bytes 196612
  238.4 8.3 %copy-start.3 = (bf16[128,256]{0,1:T(8,128)(2,1)S(1)}, bf16[128,256]{0,1:T(8,128)(2,1)}, u32[]{:S(2)}) copy-start(bf16[128,256]{0,1:T(8,128)(2,1)} %copy.235) | copy-start | bytes 196612
  256.8 6.3 %copy-start.54 = (f32[128,4]{0,1:T(4,128)}, f32[128,4]{0,1:T(4,128)S(1)}, u32[]{:S(2)}) copy-start(f32[128,4]{0,1:T(4,128)S(1)} %get-tuple-element.2318) | copy-start | bytes 6148
  256.8 6.3 %copy-start.72 = (f32[128,4]{0,1:T(4,128)}, f32[128,4]{0,1:T(4,128)S(1)}, u32[]{:S(2)}) copy-start(f32[128,4]{0,1:T(4,128)S(1)} %get-tuple-element.2345) | copy-start | bytes 6148
  288.5 27.2 %copy-start.41 = (f32[128,4,32]{0,2,1:T(8,128)S(1)}, f32[128,4,32]{0,2,1:T(8,128)}, u32[]{:S(2)}) copy-start(f32[128,4,32]{0,2,1:T(8,128)} %get-tuple-element.3050) | copy-start | bytes 196612
  288.5 27.2 %copy-start.42 = (f32[128,4,32]{0,2,1:T(8,128)S(1)}, f32[128,4,32]{0,2,1:T(8,128)}, u32[]{:S(2)}) copy-start(f32[128,4,32]{0,2,1:T(8,128)} %get-tuple-element.3060) | copy-start | bytes 196612
  288.5 27.2 %copy-start.43 = (f32[128,4,32]{0,2,1:T(8,128)S(1)}, f32[128,4,32]{0,2,1:T(8,128)}, u32[]{:S(2)}) copy-start(f32[128,4,32]{0,2,1:T(8,128)} %get-tuple-element.3058) | copy-start | bytes 196612
  288.5 32.1 %copy-start.40 = (f32[128,4,32]{0,2,1:T(8,128)S(1)}, f32[128,4,32]{0,2,1:T(8,128)}, u32[]{:S(2)}) copy-start(f32[128,4,32]{0,2,1:T(8,128)} %get-tuple-element.3032) | copy-start | bytes 196612
  290.4 51.8 %copy-start.39 = (f32[128,4,128]{0,2,1:T(8,128)S(1)}, f32[128,4,128]{0,2,1:T(8,128)}, u32[]{:S(2)}) copy-start(f32[128,4,128]{0,2,1:T(8,128)} %copy.239) | copy-start | bytes 786436
  290.4 56.4 %copy-start.38 = (f32[128,4,128]{0,2,1:T(8,128)S(1)}, f32[128,4,128]{0,2,1:T(8,128)}, u32[]{:S(2)}) copy-start(f32[128,4,128]{0,2,1:T(8,128)} %copy.251) | copy-start | bytes 786436
  290.4 61.1 %copy-start.37 = (f32[128,4,128]{0,2,1:T(8,128)S(1)}, f32[128,4,128]{0,2,1:T(8,128)}, u32[]{:S(2)}) copy-start(f32[128,4,128]{0,2,1:T(8,128)} %copy.263) | copy-start | bytes 786436
  290.4 65.8 %copy-start.36 = (f32[128,4,128]{0,2,1:T(8,128)S(1)}, f32[128,4,128]{0,2,1:T(8,128)}, u32[]{:S(2)}) copy-start(f32[128,4,128]{0,2,1:T(8,128)} %copy.275) | copy-start | bytes 786436
  293.4 34.9 %copy-start.76 = (f32[128,4]{0,1:T(4,128)}, f32[128,4]{0,1:T(4,128)S(1)}, u32[]{:S(2)}) copy-start(f32[128,4]{0,1:T(4,128)S(1)} %max.143) | copy-start | bytes 6148
  294.8 33.6 %copy-start.78 = (f32[128,4]{0,1:T(4,128)}, f32[128,4]{0,1:T(4,128)S(1)}, u32[]{:S(2)}) copy-start(f32[128,4]{0,1:T(4,128)S(1)} %max.142) | copy-start | bytes 6148
  295.5 32.9 %copy-start.80 = (f32[128,4]{0,1:T(4,128)}, f32[128,4]{0,1:T(4,128)S(1)}, u32[]{:S(2)}) copy-start(f32[128,4]{0,1:T(4,128)S(1)} %max.141) | copy-start | bytes 6148
  296.1 32.2 %copy-start.82 = (f32[128,4]{0,1:T(4,128)}, f32[128,4]{0,1:T(4,128)S(1)}, u32[]{:S(2)}) copy-start(f32[128,4]{0,1:T(4,128)S(1)} %max.140) | copy-start | bytes 6148
  296.8 35.3 %copy-start.84 = (f32[128,4]{0,1:T(4,128)}, f32[128,4]{0,1:T(4,128)S(1)}, u32[]{:S(2)}) copy-start(f32[128,4]{0,1:T(4,128)S(1)} %max.139) | copy-start | bytes 6148
  297.5 34.6 %copy-start.86 = (f32[128,4]{0,1:T(4,128)}, f32[128,4]{0,1:T(4,128)S(1)}, u32[]{:S(2)}) copy-start(f32[128,4]{0,1:T(4,128)S(1)} %max.138) | copy-start | bytes 6148
  298.2 33.9 %copy-start.87 = (f32[128,4]{0,1:T(4,128)}, f32[128,4]{0,1:T(4,128)S(1)}, u32[]{:S(2)}) copy-start(f32[128,4]{0,1:T(4,128)S(1)} %max.137) | copy-start | bytes 6148
  298.9 33.2 %copy-start.88 = (f32[128,4]{0,1:T(4,128)}, f32[128,4]{0,1:T(4,128)S(1)}, u32[]{:S(2)}) copy-start(f32[128,4]{0,1:T(4,128)S(1)} %max.136) | copy-start | bytes 6148
  299.6 32.5 %copy-start.89 = (f32[128,4]{0,1:T(4,128)}, f32[128,4]{0,1:T(4,128)S(1)}, u32[]{:S(2)}) copy-start(f32[128,4]{0,1:T(4,128)S(1)} %max.135) | copy-start | bytes 6148
  300.3 31.9 %copy-start.90 = (f32[128,4]{0,1:T(4,128)}, f32[128,4]{0,1:T(4,128)S(1)}, u32[]{:S(2)}) copy-start(f32[128,4]{0,1:T(4,128)S(1)} %max.134) | copy-start | bytes 6148
  300.9 31.2 %copy-start.91 = (f32[128,4]{0,1:T(4,128)}, f32[128,4]{0,1:T(4,128)S(1)}, u32[]{:S(2)}) copy-start(f32[128,4]{0,1:T(4,128)S(1)} %max.133) | copy-start | bytes 6148
  301.7 30.5 %copy-start.92 = (f32[128,4]{0,1:T(4,128)}, f32[128,4]{0,1:T(4,128)S(1)}, u32[]{:S(2)}) copy-start(f32[128,4]{0,1:T(4,128)S(1)} %max.132) | copy-start | bytes 6148
  315.6 42.1 %copy-start.35 = (f32[128,4,128]{0,2,1:T(8,128)S(1)}, f32[128,4,128]{0,2,1:T(8,128)}, u32[]{:S(2)}) copy-start(f32[128,4,128]{0,2,1:T(8,128)} %copy.281) | copy-start | bytes 786436
  327.0 32.3 %copy-start.33 = (f32[128,4,128]{0,2,1:T(8,128)S(1)}, f32[128,4,128]{0,2,1:T(8,128)}, u32[]{:S(2)}) copy-start(f32[128,4,128]{0,2,1:T(8,128)} %copy.287) | copy-start | bytes 786436
  328.3 30.9 %copy-start.77 = (f32[128,4]{0,1:T(4,128)S(1)}, f32[128,4]{0,1:T(4,128)}, u32[]{:S(2)}) copy-start(f32[128,4]{0,1:T(4,128)} %copy-done.76) | copy-start | bytes 6148
  329.2 82.7 %reduce-scatter.3.cloned.1.call-start = ((), (), s32[]{:S(2)}) async-start(), calls=%async_computation.4 | async-start | bytes 2621440 | tf_op jit(solution)/shard_map/reduce_scatter | solution.py:149
  329.2 17.6 %copy-start.100 = (f32[128,4]{0,1:T(4,128)S(1)}, f32[128,4]{0,1:T(4,128)}, u32[]{:S(2)}) copy-start(f32[128,4]{0,1:T(4,128)} %get-tuple-element.3064) | copy-start | bytes 6148
  329.2 20.0 %copy-start.99 = (f32[128,4]{0,1:T(4,128)S(1)}, f32[128,4]{0,1:T(4,128)}, u32[]{:S(2)}) copy-start(f32[128,4]{0,1:T(4,128)} %get-tuple-element.2950) | copy-start | bytes 6148
  329.2 22.3 %copy-start.97 = (f32[128,4]{0,1:T(4,128)S(1)}, f32[128,4]{0,1:T(4,128)}, u32[]{:S(2)}) copy-start(f32[128,4]{0,1:T(4,128)} %get-tuple-element.3076) | copy-start | bytes 6148
  329.2 24.6 %copy-start.83 = (f32[128,4]{0,1:T(4,128)S(1)}, f32[128,4]{0,1:T(4,128)}, u32[]{:S(2)}) copy-start(f32[128,4]{0,1:T(4,128)} %copy-done.82) | copy-start | bytes 6148
  329.2 24.6 %copy-start.95 = (f32[128,4]{0,1:T(4,128)S(1)}, f32[128,4]{0,1:T(4,128)}, u32[]{:S(2)}) copy-start(f32[128,4]{0,1:T(4,128)} %get-tuple-element.2946) | copy-start | bytes 6148
  329.3 27.0 %copy-start.81 = (f32[128,4]{0,1:T(4,128)S(1)}, f32[128,4]{0,1:T(4,128)}, u32[]{:S(2)}) copy-start(f32[128,4]{0,1:T(4,128)} %copy-done.80) | copy-start | bytes 6148
  329.3 27.0 %copy-start.96 = (f32[128,4]{0,1:T(4,128)S(1)}, f32[128,4]{0,1:T(4,128)}, u32[]{:S(2)}) copy-start(f32[128,4]{0,1:T(4,128)} %get-tuple-element.3074) | copy-start | bytes 6148
  329.3 28.4 %copy-start.79 = (f32[128,4]{0,1:T(4,128)S(1)}, f32[128,4]{0,1:T(4,128)}, u32[]{:S(2)}) copy-start(f32[128,4]{0,1:T(4,128)} %copy-done.78) | copy-start | bytes 6148
  329.3 28.4 %copy-start.94 = (f32[128,4]{0,1:T(4,128)S(1)}, f32[128,4]{0,1:T(4,128)}, u32[]{:S(2)}) copy-start(f32[128,4]{0,1:T(4,128)} %get-tuple-element.2942) | copy-start | bytes 6148
  330.8 30.6 %copy-start.34 = (f32[128,4,128]{0,2,1:T(8,128)S(1)}, f32[128,4,128]{0,2,1:T(8,128)}, u32[]{:S(2)}) copy-start(f32[128,4,128]{0,2,1:T(8,128)} %copy.293) | copy-start | bytes 786436
  330.8 30.6 %copy-start.93 = (f32[128,4]{0,1:T(4,128)S(1)}, f32[128,4]{0,1:T(4,128)}, u32[]{:S(2)}) copy-start(f32[128,4]{0,1:T(4,128)} %get-tuple-element.2938) | copy-start | bytes 6148
  333.4 18.1 %copy-start.85 = (f32[128,4]{0,1:T(4,128)S(1)}, f32[128,4]{0,1:T(4,128)}, u32[]{:S(2)}) copy-start(f32[128,4]{0,1:T(4,128)} %copy-done.84) | copy-start | bytes 6148
  333.4 29.5 %copy-start.32 = (f32[128,4,128]{0,2,1:T(8,128)S(1)}, f32[128,4,128]{0,2,1:T(8,128)}, u32[]{:S(2)}) copy-start(f32[128,4,128]{0,2,1:T(8,128)} %copy.299) | copy-start | bytes 786436
  333.4 29.5 %copy-start.98 = (f32[128,4]{0,1:T(4,128)S(1)}, f32[128,4]{0,1:T(4,128)}, u32[]{:S(2)}) copy-start(f32[128,4]{0,1:T(4,128)} %get-tuple-element.2936) | copy-start | bytes 6148
  334.7 28.5 %copy-start.61 = (f32[128,64]{0,1:T(8,128)S(1)}, f32[128,64]{0,1:T(8,128)}, u32[]{:S(2)}) copy-start(f32[128,64]{0,1:T(8,128)} %get-tuple-element.2934) | copy-start | bytes 98308
  (41 other events, 161.3 us)
Sparse Core Ops, SparseCore 0:
  9.1 69.0 all-gather.2
  80.0 64.3 all-gather.4
  329.3 32.8 reduce-scatter.4
  367.0 44.8 reduce-scatter.2
where the time goes:
time: 426 us; the launch traced here: 421 us
  waiting for transfers between devices  151 us (35%)
  matrix products  151 us (35%)
  local copies, waits for them, and re-layouts  44.5 us (10%)
  other arithmetic  43.7 us (10%)
  between operations  16.3 us (4%)
  blocking collectives  12.5 us (3%)
    all_gather x1, waiting for transfers between devices, shards(): lax.all_gather(w_value, 'ctx', axis=1, tiled=True)  61.9 us
    reduce_scatter x1, waiting for transfers between devices, shards(): lax.psum_scatter((running_out * factor[..., None]).reshape(query_count, H...  44.2 us
    all_gather x1, waiting for transfers between devices, shards(): lax.all_gather(w_key, 'ctx', axis=1, tiled=True)  43.7 us
    dot_general x32, matrix products, expand_block(): jnp.dot(lat_rows, weight_value, preferred_element_type=jnp.float32)  41.1 us
    dot_general x32, matrix products, expand_block(): jnp.dot(lat_rows, weight_key, preferred_element_type=jnp.float32)  41 us
    dot_general x32, matrix products, expand_block(): jnp.einsum('qhd,kd->qhk', query_rope, rope_keys, preferred_element_type=j...  32.5 us
    while x32, local copies, waits for them, and re-layouts, cached_pass(): return lax.fori_loop(0, block_count, advance, running)  22 us
    dot_general x32, matrix products, expand_block(): jnp.einsum('qhk,khd->qhd', weights.astype(jnp.bfloat16), value_rows, pref...  20.2 us
  transfers between devices with their start and end apart: 4, of which 3 were waited for; matrix products, arithmetic and copies ran while one was open for 16% of the time, Pallas kernels for 0%

commit v1 on v0

v1 whole, which is shorter than its diff:
```python
import functools
import math

import jax
import jax.numpy as jnp
from jax import lax
from jax.experimental import pallas as pl
from jax.experimental.pallas import tpu as pltpu
from jax.sharding import PartitionSpec as P

DC = 512
DR = 64
DH = 128
DV = 128
HEADS = 64
CTX = 4
HERE = HEADS // CTX
PAIRS = HERE // 2
Q = 128
ROWS = 256
NEW = 32
HALF = ROWS // 2
NROW = CTX * (ROWS + NEW)
KEXT = DC + 128
LOG2E = 1.4426950408889634
SCALE = LOG2E / math.sqrt(DH + DR)
BLOCKED = -1e30
MESH = pl.DeviceIdType.MESH
F32 = jnp.float32
BF16 = jnp.bfloat16

NEW0 = CTX * ROWS
SLOT_ROWS = (
    ((0, 0, ROWS),),
    ((ROWS, 0, ROWS),),
    ((2 * ROWS, 0, HALF), (3 * ROWS, HALF, HALF)),
    ((2 * ROWS + HALF, 0, HALF), (3 * ROWS + HALF, HALF, HALF)),
)


def kernel(
    qn_hbm, qr_hbm, cl_hbm, cr_hbm, nl_hbm, nr_hbm, len_hbm, wk_hbm, wv_hbm, o_hbm,
    qn, qr, wk, wv, lat, rope, nrope, lens, ext, latt, qt, acc, top, total, out,
    load_sem, out_sem, sib_send, sib_recv, par_send, par_recv, fwd_send, fwd_recv,
):
    me = lax.axis_index("ctx")
    sib = me + 1 - 2 * lax.rem(me, 2)
    par = lax.rem(me + 2, CTX)
    far = lax.rem(sib + 2, CTX)

    def local(index, src, dst):
        return pltpu.make_async_copy(src, dst, load_sem.at[index])

    loads = dict(
        wk=local(0, wk_hbm, wk),
        qn=local(1, qn_hbm.at[0, :, pl.ds(pl.multiple_of(me * HERE * DH, HERE * DH), HERE * DH)], qn),
        qr=local(2, qr_hbm.at[0, :, pl.ds(pl.multiple_of(me * HERE * DR, HERE * DR), HERE * DR)], qr),
        cl=local(3, cl_hbm.at[0], lat.at[pl.ds(0, ROWS)]),
        cr=local(4, cr_hbm.at[0], rope.at[0]),
        nl=local(5, nl_hbm.at[0], lat.at[pl.ds(NEW0, NEW)]),
        nr=local(6, nr_hbm.at[0], nrope.at[0]),
        ln=local(7, len_hbm, lens.at[0]),
        wv=local(8, wv_hbm, wv),
    )
    barrier = pltpu.get_barrier_semaphore()
    for peer in (sib, par):
        pl.semaphore_signal(barrier, inc=1, device_id={"ctx": peer}, device_id_type=MESH)
    for name in ("wk", "qn", "qr", "cl", "cr", "nl", "nr", "ln", "wv"):
        loads[name].start()
    pl.semaphore_wait(barrier, 2)

    def remote(src, dst, send, recv, index, peer):
        return pltpu.make_async_remote_copy(
            src_ref=src, dst_ref=dst, send_sem=send.at[index], recv_sem=recv.at[index],
            device_id={"ctx": peer}, device_id_type=MESH,
        )

    def small(slot):
        return (
            rope.at[slot], lens.at[slot], nrope.at[slot], lat.at[pl.ds(NEW0 + slot * NEW, NEW)],
        )

    mine = (cr_hbm.at[0], len_hbm, nr_hbm.at[0], nl_hbm.at[0])
    halves = tuple(cl_hbm.at[0, pl.ds(HALF * k, HALF)] for k in range(2))

    def landed(slot):
        return tuple(lat.at[pl.ds(row, count)] for row, _, count in SLOT_ROWS[slot])

    to_par = [
        remote(src, dst, par_send, par_recv, k, par)
        for k, (src, dst) in enumerate(zip(mine + halves, small(2) + landed(2)))
    ]
    to_sib = [
        remote(src, dst, sib_send, sib_recv, k, sib)
        for k, (src, dst) in enumerate(zip(mine + (cl_hbm.at[0],), small(1) + landed(1)))
    ]
    forward = [
        remote(src, dst, fwd_send, fwd_recv, k, sib)
        for k, (src, dst) in enumerate(zip(small(2) + landed(2), small(3) + landed(3)))
    ]
    for copy in to_par + to_sib:
        copy.start()

    top[...] = jnp.full_like(top, BLOCKED)
    total[...] = jnp.zeros_like(total)
    acc[...] = jnp.zeros_like(acc)
    row_of = lax.broadcasted_iota(jnp.int32, (KEXT - DC - DR, 2 * Q), 0)
    tail = jnp.where(row_of == 0, BLOCKED, 0.0).astype(BF16)
    for pair in range(PAIRS):
        qt[pair, DC + DR :, :] = tail

    loads["wk"].wait()
    loads["qn"].wait()
    loads["qr"].wait()
    for head in range(HERE):
        pair, side = head // 2, (head % 2) * Q
        part = lax.dot_general(
            wk[:, head * DH : (head + 1) * DH], qn[:, head * DH : (head + 1) * DH],
            (((1,), (1,)), ((), ())), preferred_element_type=F32,
        )
        qt[pair, :DC, side : side + Q] = part.astype(BF16)
    for pair in range(PAIRS):
        turned = qr[:, pair * 2 * DR : (pair + 1) * 2 * DR].T
        qt[pair, DC : DC + DR, :Q] = turned[:DR]
        qt[pair, DC : DC + DR, Q:] = turned[DR:]

    lane = lax.broadcasted_iota(jnp.int32, (ROWS, KEXT - DC), 1)
    row = lax.broadcasted_iota(jnp.int32, (ROWS, KEXT - DC), 0)

    def widen(rotary, live):
        padded = jnp.concatenate([rotary, jnp.zeros_like(rotary)], axis=1).astype(F32)
        if live is not None:
            padded = jnp.where((lane == DR) & (row >= live), 1.0, padded)
        return padded.astype(BF16)

    def prepare_small(slot):
        wide = widen(rope[slot], jnp.broadcast_to(lens[slot], (ROWS, KEXT - DC)))
        for begin, first, count in SLOT_ROWS[slot]:
            ext[begin : begin + count, :] = wide[first : first + count]
        begin = NEW0 + slot * NEW
        ext[begin : begin + NEW, :] = widen(nrope[slot], None)

    def turn(begin, count):
        latt[:, begin : begin + count] = lat[begin : begin + count, :].T

    def step(pair, begin, count, fresh):
        keys = jnp.concatenate(
            [lat[begin : begin + count, :], ext[begin : begin + count, :]], axis=1
        )
        scores = jnp.dot(keys, qt[pair], preferred_element_type=F32)
        if fresh is not None:
            scores = jnp.concatenate(
                [scores[: NEW0 - begin], jnp.where(fresh, scores[NEW0 - begin :], BLOCKED)], axis=0
            )
        old = top[pair]
        level = jnp.maximum(old, jnp.max(scores, axis=0, keepdims=True))
        factor = jnp.exp2((old - level) * SCALE)
        weights = jnp.exp2((scores - level) * SCALE)
        top[pair] = level
        total[pair] = total[pair] * factor + jnp.sum(weights, axis=0, keepdims=True)
        acc[pair] = acc[pair] * factor + jnp.dot(
            latt[:, begin : begin + count], weights.astype(BF16), preferred_element_type=F32
        )

    def steps(first, last, begin, count, fresh=None):
        def body(pair, carry):
            step(pair, begin, count, fresh)
            return carry

        lax.fori_loop(first, last, body, 0, unroll=2)

    for name in ("cl", "cr", "nl", "nr", "ln"):
        loads[name].wait()
    for copy in to_sib:
        copy.wait_recv()
    prepare_small(0)
    prepare_small(1)
    turn(0, 2 * ROWS)
    steps(0, PAIRS // 2, 0, 2 * ROWS)
    for arrived, onward in zip(to_par[:5], forward[:5]):
        arrived.wait_recv()
        onward.start()
    prepare_small(2)
    turn(2 * ROWS, HALF)
    steps(PAIRS // 2, PAIRS, 0, 2 * ROWS)
    for copy in forward[:5]:
        copy.wait_recv()
    prepare_small(3)
    turn(2 * ROWS + HALF, HALF)
    steps(0, PAIRS // 2, 2 * ROWS, ROWS)
    to_par[5].wait_recv()
    forward[5].start()
    steps(PAIRS // 2, PAIRS, 2 * ROWS, ROWS)
    forward[5].wait_recv()
    turn(3 * ROWS, ROWS + CTX * NEW)
    local_row = lax.broadcasted_iota(jnp.int32, (CTX * NEW, 2 * Q), 0)
    query = lax.rem(lax.broadcasted_iota(jnp.int32, (CTX * NEW, 2 * Q), 1), Q)
    slot_of = lax.div(local_row, NEW)
    owner = jnp.where(
        slot_of == 0, me, jnp.where(slot_of == 1, sib, jnp.where(slot_of == 2, par, far))
    )
    fresh = owner * NEW + lax.rem(local_row, NEW) <= query
    steps(0, PAIRS, 3 * ROWS, ROWS + CTX * NEW, fresh)

    loads["wv"].wait()
    for pair in range(PAIRS):
        mean = (acc[pair] * (1.0 / total[pair])).astype(BF16)
        for side in range(2):
            head = 2 * pair + side
            out[:, head * DV : (head + 1) * DV] = lax.dot_general(
                mean[:, side * Q : (side + 1) * Q], wv[:, head * DV : (head + 1) * DV],
                (((0,), (0,)), ((), ())), preferred_element_type=F32,
            ).astype(BF16)
    for copy in to_par + to_sib + forward:
        copy.wait_send()
    store = pltpu.make_async_copy(out, o_hbm.at[0], out_sem)
    store.start()
    store.wait()


def shards(*operands):
    return pl.pallas_call(
        kernel,
        out_shape=jax.ShapeDtypeStruct((1, Q, HERE * DV), BF16),
        in_specs=[pl.BlockSpec(memory_space=pltpu.HBM)] * 9,
        out_specs=pl.BlockSpec(memory_space=pltpu.HBM),
        scratch_shapes=[
            pltpu.VMEM((Q, HERE * DH), BF16),
            pltpu.VMEM((Q, HERE * DR), BF16),
            pltpu.VMEM((DC, HERE * DH), BF16),
            pltpu.VMEM((DC, HERE * DV), BF16),
            pltpu.VMEM((NROW, DC), BF16),
            pltpu.VMEM((CTX, ROWS, DR), BF16),
            pltpu.VMEM((CTX, NEW, DR), BF16),
            pltpu.VMEM((CTX, 1, 1), jnp.int32),
            pltpu.VMEM((NROW, KEXT - DC), BF16),
            pltpu.VMEM((DC, NROW), BF16),
            pltpu.VMEM((PAIRS, KEXT, 2 * Q), BF16),
            pltpu.VMEM((PAIRS, DC, 2 * Q), F32),
            pltpu.VMEM((PAIRS, 1, 2 * Q), F32),
            pltpu.VMEM((PAIRS, 1, 2 * Q), F32),
            pltpu.VMEM((Q, HERE * DV), BF16),
            pltpu.SemaphoreType.DMA((9,)),
            pltpu.SemaphoreType.DMA,
        ]
        + [pltpu.SemaphoreType.DMA((6,))] * 6,
        compiler_params=pltpu.CompilerParams(
            collective_id=0, has_side_effects=True, vmem_limit_bytes=60 << 20
        ),
        cost_estimate=pl.CostEstimate(
            flops=7_000_000_000, bytes_accessed=7_000_000, transcendentals=2_400_000
        ),
        name="latent_attention",
    )(*operands)


def solution(mesh):
    return jax.shard_map(
        shards,
        mesh=mesh,
        in_specs=(
            P("req", None, None),
            P("req", None, None),
            P("req", "ctx", None),
            P("req", "ctx", None),
            P("req", "ctx", None),
            P("req", "ctx", None),
            P("req", "ctx"),
            P(None, "ctx"),
            P(None, "ctx"),
        ),
        out_specs=P("req", None, "ctx"),
        check_vma=False,
    )
```

time: 426 us -> 33 us (0.08); the launches traced: 421 us -> 32.8 us
  matrix products: 151 us -> 0 us
  waiting for transfers between devices: 151 us -> 0 us
  other arithmetic: 43.7 us -> 0 us
  local copies, waits for them, and re-layouts: 44.5 us -> 3.37 us
  Pallas kernels: 0 us -> 28.8 us
  between operations: 16.3 us -> 0.66 us
  blocking collectives: 12.5 us -> 0 us
    dot_general x160 -> x0, matrix products: 151 us -> none  [the longest x32 41.1 us: expand_block(): jnp.dot(lat_rows, weight_value, preferred_element_type=jnp.float32)]
    all_gather x2 -> x0, waiting for transfers between devices: 106 us -> none  [the longest x1 61.9 us: shards(): lax.all_gather(w_value, 'ctx', axis=1, tiled=True)]
    reduce_scatter x2 -> x0, waiting for transfers between devices: 44.2 us -> none  [the longest x1 44.2 us: shards(): lax.psum_scatter((running_out * factor[..., None]).reshape(query_count, H...]
    pallas_call x0 -> x1, Pallas kernels: none -> 28.8 us  [shards(): pl.pallas_call(kernel, out_shape=jax.ShapeDtypeStruct((1, Q, HERE * DV),...]
    while x47 -> x0, local copies, waits for them, and re-layouts: 22.6 us -> none  [the longest x32 22 us: cached_pass(): return lax.fori_loop(0, block_count, advance, running)]
    add x25 -> x0, other arithmetic: 13.1 us -> none  [the longest x24 13.1 us: expand_block(): running_sum = running_sum * factor + jnp.sum(weights, axis=-1)]
    pmax x1 -> x0, blocking collectives: 12.5 us -> none  [shards(): lax.pmax(running_max.astype(jnp.bfloat16), 'ctx').astype(running_max.dtype)]
    max x32 -> x0, other arithmetic: 11.7 us -> none  [expand_block(): new_max = jnp.maximum(running_max, jnp.max(scores, axis=-1))]
  transfers between devices with their start and end apart: 4 -> 0, of which waited for: 3 -> 0; matrix products, arithmetic and copies ran while one was open for 16% -> 0% of each run, Pallas kernels for 0% -> 0%
where the time goes in v1:
time: 33 us; the launch traced here: 32.8 us
  Pallas kernels  28.8 us (87%)
  local copies, waits for them, and re-layouts  3.37 us (10%)
  between operations  0.66 us (2%)
    pallas_call x1, Pallas kernels, shards(): pl.pallas_call(kernel, out_shape=jax.ShapeDtypeStruct((1, Q, HERE * DV),...  28.8 us
    unnamed x2, local copies, waits for them, and re-layouts  3.37 us

profile of v1, /device:TPU:1, one launch (start us, length us, event | category | flops | bytes accessed | tf_op | source)
XLA Modules:
  0.0 32.8 jit_solution(14074251476559110195)
XLA Ops:
  0.7 1.5 %copy.10.cr_hbm = bf16[1,256,64]{2,1,0:T(8,128)(2,1)} copy(bf16[1,256,64]{1,2,0:T(8,128)(2,1)} %param.12) | data formatting | bytes 65536 | tf_op args[3]
  2.1 28.8 %latent_attention.1 = bf16[1,128,2048]{2,1,0:T(8,128)(2,1)} custom-call(bf16[1,128,8192]{2,1,0:T(8,128)(2,1)} %qn_hbm.1, bf16[1,128,4096]{2,1,0:T(8,128)(2,1)} %qr_hbm.1, bf16[1,256,512]{2,1,0:T(8,128)(2,1)} %cl_hbm.1, bf16[1,256,64]{2,1,0:T(8,128)(2,1)} %copy.10.cr_hbm, bf16[1,32,512]{2,1,0:T(8,128)(2,1)} %nl_hbm.1, bf16[1,32,64]{2,1,0:T(8,128)(2,1)} %nr_hbm.1, ...), custom_call_target="tpu_custom_call" | custom-call | flops 7000000000 | bytes 7000000 | tf_op jit(solution)/shard_map/latent_attention/pallas_call | solution.py:222
  31.0 1.9 %copy.13 = bf16[1,128,2048]{2,1,0:T(8,128)(2,1)} copy(bf16[1,128,2048]{2,1,0:T(8,128)(2,1)} %latent_attention.1) | data formatting | bytes 1048576

commit v2 on v1

--- a/solution.py
+++ b/solution.py
@@ -29,18 +29,22 @@
 F32 = jnp.float32
 BF16 = jnp.bfloat16
 
-NEW0 = CTX * ROWS
+NEW0 = 2 * ROWS
+FIRST = NEW0 + CTX * NEW
+SECOND = FIRST + 2 * HALF
 SLOT_ROWS = (
     ((0, 0, ROWS),),
     ((ROWS, 0, ROWS),),
-    ((2 * ROWS, 0, HALF), (3 * ROWS, HALF, HALF)),
-    ((2 * ROWS + HALF, 0, HALF), (3 * ROWS + HALF, HALF, HALF)),
+    ((FIRST, 0, HALF), (SECOND, HALF, HALF)),
+    ((FIRST + HALF, 0, HALF), (SECOND + HALF, HALF, HALF)),
 )
+CHUNKS = ((0, 2 * ROWS), (NEW0, CTX * NEW + 2 * HALF), (SECOND, 2 * HALF))
 
 
 def kernel(
     qn_hbm, qr_hbm, cl_hbm, cr_hbm, nl_hbm, nr_hbm, len_hbm, wk_hbm, wv_hbm, o_hbm,
     qn, qr, wk, wv, lat, rope, nrope, lens, ext, latt, qt, acc, top, total, out,
+    score0, score1, weight0, weight1, factor0, factor1,
     load_sem, out_sem, sib_send, sib_recv, par_send, par_recv, fwd_send, fwd_recv,
 ):
     me = lax.axis_index("ctx")
@@ -77,10 +81,10 @@
 
     def small(slot):
         return (
-            rope.at[slot], lens.at[slot], nrope.at[slot], lat.at[pl.ds(NEW0 + slot * NEW, NEW)],
-        )
-
-    mine = (cr_hbm.at[0], len_hbm, nr_hbm.at[0], nl_hbm.at[0])
+            nrope.at[slot], lat.at[pl.ds(NEW0 + slot * NEW, NEW)], lens.at[slot], rope.at[slot],
+        )
+
+    mine = (nr_hbm.at[0], nl_hbm.at[0], len_hbm, cr_hbm.at[0])
     halves = tuple(cl_hbm.at[0, pl.ds(HALF * k, HALF)] for k in range(2))
 
     def landed(slot):
@@ -101,9 +105,6 @@
     for copy in to_par + to_sib:
         copy.start()
 
-    top[...] = jnp.full_like(top, BLOCKED)
-    total[...] = jnp.zeros_like(total)
-    acc[...] = jnp.zeros_like(acc)
     row_of = lax.broadcasted_iota(jnp.int32, (KEXT - DC - DR, 2 * Q), 0)
     tail = jnp.where(row_of == 0, BLOCKED, 0.0).astype(BF16)
     for pair in range(PAIRS):
@@ -124,75 +125,25 @@
         qt[pair, DC : DC + DR, :Q] = turned[:DR]
         qt[pair, DC : DC + DR, Q:] = turned[DR:]
 
-    lane = lax.broadcasted_iota(jnp.int32, (ROWS, KEXT - DC), 1)
-    row = lax.broadcasted_iota(jnp.int32, (ROWS, KEXT - DC), 0)
-
-    def widen(rotary, live):
-        padded = jnp.concatenate([rotary, jnp.zeros_like(rotary)], axis=1).astype(F32)
-        if live is not None:
-            padded = jnp.where((lane == DR) & (row >= live), 1.0, padded)
-        return padded.astype(BF16)
-
-    def prepare_small(slot):
-        wide = widen(rope[slot], jnp.broadcast_to(lens[slot], (ROWS, KEXT - DC)))
+    lane = lax.broadcasted_iota(jnp.int32, (DR, ROWS), 1)
+    row = lax.broadcasted_iota(jnp.int32, (DR, ROWS), 0)
+
+    def prepare_new(slot):
+        begin = NEW0 + slot * NEW
+        ext[begin : begin + NEW, :] = jnp.concatenate(
+            [nrope[slot], jnp.zeros((NEW, KEXT - DC - DR), BF16)], axis=1
+        )
+
+    def prepare_cached(slot):
+        live = jnp.broadcast_to(lens[slot], (DR, ROWS))
+        dead = jnp.where((row == 0) & (lane >= live), 1.0, 0.0).astype(BF16)
+        wide = jnp.concatenate([rope[slot], dead], axis=0).T
         for begin, first, count in SLOT_ROWS[slot]:
             ext[begin : begin + count, :] = wide[first : first + count]
-        begin = NEW0 + slot * NEW
-        ext[begin : begin + NEW, :] = widen(nrope[slot], None)
 
     def turn(begin, count):
         latt[:, begin : begin + count] = lat[begin : begin + count, :].T
 
-    def step(pair, begin, count, fresh):
-        keys = jnp.concatenate(
-            [lat[begin : begin + count, :], ext[begin : begin + count, :]], axis=1
-        )
-        scores = jnp.dot(keys, qt[pair], preferred_element_type=F32)
-        if fresh is not None:
-            scores = jnp.concatenate(
-                [scores[: NEW0 - begin], jnp.where(fresh, scores[NEW0 - begin :], BLOCKED)], axis=0
-            )
-        old = top[pair]
-        level = jnp.maximum(old, jnp.max(scores, axis=0, keepdims=True))
-        factor = jnp.exp2((old - level) * SCALE)
-        weights = jnp.exp2((scores - level) * SCALE)
-        top[pair] = level
-        total[pair] = total[pair] * factor + jnp.sum(weights, axis=0, keepdims=True)
-        acc[pair] = acc[pair] * factor + jnp.dot(
-            latt[:, begin : begin + count], weights.astype(BF16), preferred_element_type=F32
-        )
-
-    def steps(first, last, begin, count, fresh=None):
-        def body(pair, carry):
-            step(pair, begin, count, fresh)
-            return carry
-
-        lax.fori_loop(first, last, body, 0, unroll=2)
-
-    for name in ("cl", "cr", "nl", "nr", "ln"):
-        loads[name].wait()
-    for copy in to_sib:
-        copy.wait_recv()
-    prepare_small(0)
-    prepare_small(1)
-    turn(0, 2 * ROWS)
-    steps(0, PAIRS // 2, 0, 2 * ROWS)
-    for arrived, onward in zip(to_par[:5], forward[:5]):
-        arrived.wait_recv()
-        onward.start()
-    prepare_small(2)
-    turn(2 * ROWS, HALF)
-    steps(PAIRS // 2, PAIRS, 0, 2 * ROWS)
-    for copy in forward[:5]:
-        copy.wait_recv()
-    prepare_small(3)
-    turn(2 * ROWS + HALF, HALF)
-    steps(0, PAIRS // 2, 2 * ROWS, ROWS)
-    to_par[5].wait_recv()
-    forward[5].start()
-    steps(PAIRS // 2, PAIRS, 2 * ROWS, ROWS)
-    forward[5].wait_recv()
-    turn(3 * ROWS, ROWS + CTX * NEW)
     local_row = lax.broadcasted_iota(jnp.int32, (CTX * NEW, 2 * Q), 0)
     query = lax.rem(lax.broadcasted_iota(jnp.int32, (CTX * NEW, 2 * Q), 1), Q)
     slot_of = lax.div(local_row, NEW)
@@ -200,7 +151,83 @@
         slot_of == 0, me, jnp.where(slot_of == 1, sib, jnp.where(slot_of == 2, par, far))
     )
     fresh = owner * NEW + lax.rem(local_row, NEW) <= query
-    steps(0, PAIRS, 3 * ROWS, ROWS + CTX * NEW, fresh)
+
+    score, weight, factor = (score0, score1), (weight0, weight1), (factor0, factor1)
+    items = [(chunk, pair) for chunk in range(len(CHUNKS)) for pair in range(PAIRS)]
+
+    def score_of(index):
+        chunk, pair = items[index]
+        begin, count = CHUNKS[chunk]
+        keys = jnp.concatenate(
+            [lat[begin : begin + count, :], ext[begin : begin + count, :]], axis=1
+        )
+        score[index % 2][:count] = jnp.dot(keys, qt[pair], preferred_element_type=F32)
+
+    def weigh(index):
+        chunk, pair = items[index]
+        begin, count = CHUNKS[chunk]
+        scores = score[index % 2][:count]
+        if begin == NEW0:
+            new = CTX * NEW
+            scores = jnp.concatenate([jnp.where(fresh, scores[:new], BLOCKED), scores[new:]], axis=0)
+        level = jnp.max(scores, axis=0, keepdims=True)
+        if chunk:
+            level = jnp.maximum(top[pair], level)
+            change = jnp.exp2((top[pair] - level) * SCALE)
+            factor[index % 2][...] = change
+        weights = jnp.exp2((scores - level) * SCALE)
+        sums = jnp.sum(weights, axis=0, keepdims=True)
+        top[pair] = level
+        total[pair] = total[pair] * change + sums if chunk else sums
+        weight[index % 2][:count] = weights.astype(BF16)
+
+    def gather_in(index):
+        chunk, pair = items[index]
+        begin, count = CHUNKS[chunk]
+        part = jnp.dot(
+            latt[:, begin : begin + count], weight[index % 2][:count], preferred_element_type=F32
+        )
+        acc[pair] = acc[pair] * factor[index % 2][...] + part if chunk else part
+
+    def onward(indices):
+        for k in indices:
+            to_par[k].wait_recv()
+            forward[k].start()
+
+    def before_item(index):
+        if index == 0:
+            for name in ("cl", "cr", "nl", "nr", "ln"):
+                loads[name].wait()
+            for copy in to_sib:
+                copy.wait_recv()
+            for slot in range(2):
+                prepare_new(slot)
+                prepare_cached(slot)
+            turn(0, NEW0)
+        if index == 3:
+            onward(range(4))
+        if index == PAIRS:
+            onward(range(4, 5))
+            for copy in forward[:5]:
+                copy.wait_recv()
+            for slot in range(2, 4):
+                prepare_new(slot)
+                prepare_cached(slot)
+            turn(NEW0, SECOND - NEW0)
+        if index == 2 * PAIRS - 3:
+            onward(range(5, 6))
+        if index == 2 * PAIRS:
+            forward[5].wait_recv()
+            turn(SECOND, NROW - SECOND)
+
+    for index in range(len(items) + 2):
+        if index < len(items):
+            before_item(index)
+            score_of(index)
+        if 1 <= index <= len(items):
+            weigh(index - 1)
+        if index >= 2:
+            gather_in(index - 2)
 
     loads["wv"].wait()
     for pair in range(PAIRS):
@@ -219,6 +246,7 @@
 
 
 def shards(*operands):
+    operands = operands[:3] + (jnp.swapaxes(operands[3], 1, 2),) + operands[4:]
     return pl.pallas_call(
         kernel,
         out_shape=jax.ShapeDtypeStruct((1, Q, HERE * DV), BF16),
@@ -230,7 +258,7 @@
             pltpu.VMEM((DC, HERE * DH), BF16),
             pltpu.VMEM((DC, HERE * DV), BF16),
             pltpu.VMEM((NROW, DC), BF16),
-            pltpu.VMEM((CTX, ROWS, DR), BF16),
+            pltpu.VMEM((CTX, DR, ROWS), BF16),
             pltpu.VMEM((CTX, NEW, DR), BF16),
             pltpu.VMEM((CTX, 1, 1), jnp.int32),
             pltpu.VMEM((NROW, KEXT - DC), BF16),
@@ -240,6 +268,12 @@
             pltpu.VMEM((PAIRS, 1, 2 * Q), F32),
             pltpu.VMEM((PAIRS, 1, 2 * Q), F32),
             pltpu.VMEM((Q, HERE * DV), BF16),
+            pltpu.VMEM((2 * ROWS, 2 * Q), F32),
+            pltpu.VMEM((2 * ROWS, 2 * Q), F32),
+            pltpu.VMEM((2 * ROWS, 2 * Q), BF16),
+            pltpu.VMEM((2 * ROWS, 2 * Q), BF16),
+            pltpu.VMEM((1, 2 * Q), F32),
+            pltpu.VMEM((1, 2 * Q), F32),
             pltpu.SemaphoreType.DMA((9,)),
             pltpu.SemaphoreType.DMA,
         ]

time: 33 us -> 23 us (0.70)
  Pallas kernels: 28.8 us -> 20.3 us
  local copies, waits for them, and re-layouts: 3.37 us -> 1.88 us
    pallas_call x1, Pallas kernels: 28.8 us -> 20.3 us  [shards(): pl.pallas_call(kernel, out_shape=jax.ShapeDtypeStruct((1, Q, HERE * DV),...]
    unnamed x2 -> x1, local copies, waits for them, and re-layouts: 3.37 us -> 1.88 us
where the time goes in v2:
time: 23 us; the launch traced here: 22.9 us
  Pallas kernels  20.3 us (88%)
  local copies, waits for them, and re-layouts  1.88 us (8%)
  between operations  0.66 us (3%)
    pallas_call x1, Pallas kernels, shards(): pl.pallas_call(kernel, out_shape=jax.ShapeDtypeStruct((1, Q, HERE * DV),...  20.3 us
    unnamed x1, local copies, waits for them, and re-layouts  1.88 us

profile of v2, /device:TPU:1, one launch (start us, length us, event | category | flops | bytes accessed | tf_op | source)
XLA Modules:
  0.0 22.9 jit_solution(6847141261468124933)
XLA Ops:
  0.7 20.3 %latent_attention.1 = bf16[1,128,2048]{2,1,0:T(8,128)(2,1)} custom-call(bf16[1,128,8192]{2,1,0:T(8,128)(2,1)} %qn_hbm.1, bf16[1,128,4096]{2,1,0:T(8,128)(2,1)} %qr_hbm.1, bf16[1,256,512]{2,1,0:T(8,128)(2,1)} %cl_hbm.1, bf16[1,64,256]{2,1,0:T(8,128)(2,1)} %bitcast.1, bf16[1,32,512]{2,1,0:T(8,128)(2,1)} %nl_hbm.1, bf16[1,32,64]{2,1,0:T(8,128)(2,1)} %nr_hbm.1, ...), custom_call_target="tpu_custom_call" | custom-call | flops 7000000000 | bytes 7000000 | tf_op jit(solution)/shard_map/latent_attention/pallas_call | solution.py:250
  21.0 1.9 %copy.12 = bf16[1,128,2048]{2,1,0:T(8,128)(2,1)} copy(bf16[1,128,2048]{2,1,0:T(8,128)(2,1)} %latent_attention.1) | data formatting | bytes 1048576

commit v3 on v2

--- a/solution.py
+++ b/solution.py
@@ -42,10 +42,10 @@
 
 
 def kernel(
-    qn_hbm, qr_hbm, cl_hbm, cr_hbm, nl_hbm, nr_hbm, len_hbm, wk_hbm, wv_hbm, o_hbm,
-    qn, qr, wk, wv, lat, rope, nrope, lens, ext, latt, qt, acc, top, total, out,
+    qn_hbm, qr_hbm, cl_hbm, cr_hbm, nl_hbm, nr_hbm, len_hbm, wk_hbm, wv_hbm, out,
+    qn, qr, wk, wv, lat, rope, nrope, lens, ext, latt, qt, acc, top, total,
     score0, score1, weight0, weight1, factor0, factor1,
-    load_sem, out_sem, sib_send, sib_recv, par_send, par_recv, fwd_send, fwd_recv,
+    load_sem, sib_send, sib_recv, par_send, par_recv, fwd_send, fwd_recv,
 ):
     me = lax.axis_index("ctx")
     sib = me + 1 - 2 * lax.rem(me, 2)
@@ -234,24 +234,25 @@
         mean = (acc[pair] * (1.0 / total[pair])).astype(BF16)
         for side in range(2):
             head = 2 * pair + side
-            out[:, head * DV : (head + 1) * DV] = lax.dot_general(
+            out[0, :, head * DV : (head + 1) * DV] = lax.dot_general(
                 mean[:, side * Q : (side + 1) * Q], wv[:, head * DV : (head + 1) * DV],
                 (((0,), (0,)), ((), ())), preferred_element_type=F32,
             ).astype(BF16)
     for copy in to_par + to_sib + forward:
         copy.wait_send()
-    store = pltpu.make_async_copy(out, o_hbm.at[0], out_sem)
-    store.start()
-    store.wait()
 
 
 def shards(*operands):
     operands = operands[:3] + (jnp.swapaxes(operands[3], 1, 2),) + operands[4:]
+    operands = tuple(
+        x if index == 6 else pltpu.with_memory_space_constraint(x, pltpu.HBM)
+        for index, x in enumerate(operands)
+    )
     return pl.pallas_call(
         kernel,
-        out_shape=jax.ShapeDtypeStruct((1, Q, HERE * DV), BF16),
+        out_shape=pltpu.VMEM((1, Q, HERE * DV), BF16),
         in_specs=[pl.BlockSpec(memory_space=pltpu.HBM)] * 9,
-        out_specs=pl.BlockSpec(memory_space=pltpu.HBM),
+        out_specs=pl.BlockSpec(memory_space=pltpu.VMEM),
         scratch_shapes=[
             pltpu.VMEM((Q, HERE * DH), BF16),
             pltpu.VMEM((Q, HERE * DR), BF16),
@@ -267,7 +268,6 @@
             pltpu.VMEM((PAIRS, DC, 2 * Q), F32),
             pltpu.VMEM((PAIRS, 1, 2 * Q), F32),
             pltpu.VMEM((PAIRS, 1, 2 * Q), F32),
-            pltpu.VMEM((Q, HERE * DV), BF16),
             pltpu.VMEM((2 * ROWS, 2 * Q), F32),
             pltpu.VMEM((2 * ROWS, 2 * Q), F32),
             pltpu.VMEM((2 * ROWS, 2 * Q), BF16),
@@ -275,11 +275,10 @@
             pltpu.VMEM((1, 2 * Q), F32),
             pltpu.VMEM((1, 2 * Q), F32),
             pltpu.SemaphoreType.DMA((9,)),
-            pltpu.SemaphoreType.DMA,
         ]
         + [pltpu.SemaphoreType.DMA((6,))] * 6,
         compiler_params=pltpu.CompilerParams(
-            collective_id=0, has_side_effects=True, vmem_limit_bytes=60 << 20
+            collective_id=0, has_side_effects=True, vmem_limit_bytes=40 << 20
         ),
         cost_estimate=pl.CostEstimate(
             flops=7_000_000_000, bytes_accessed=7_000_000, transcendentals=2_400_000

time: 23 us -> 21.1 us (0.917)
  local copies, waits for them, and re-layouts: 1.88 us -> 0.8 us
  Pallas kernels: 20.3 us -> 19.5 us
    unnamed x1, local copies, waits for them, and re-layouts: 1.88 us -> 0.8 us
    pallas_call x1, Pallas kernels: 20.3 us -> 19.5 us  [shards(): pl.pallas_call(kernel, out_shape=pltpu.VMEM((1, Q, HERE * DV), BF16), in_...]
where the time goes in v3:
time: 21.1 us; the launch traced here: 21 us
  Pallas kernels  19.5 us (92%)
  local copies, waits for them, and re-layouts  0.8 us (4%)
  between operations  0.66 us (3%)
    pallas_call x1, Pallas kernels, shards(): pl.pallas_call(kernel, out_shape=pltpu.VMEM((1, Q, HERE * DV), BF16), in_...  19.5 us
    unnamed x1, local copies, waits for them, and re-layouts  0.8 us

profile of v3, /device:TPU:1, one launch (start us, length us, event | category | flops | bytes accessed | tf_op | source)
XLA Modules:
  0.0 21.0 jit_solution(17356619699797210904)
XLA Ops:
  0.7 19.5 %latent_attention.1 = bf16[1,128,2048]{2,1,0:T(8,128)(2,1)S(1)} custom-call(bf16[1,128,8192]{2,1,0:T(8,128)(2,1)} %qn_hbm.1, bf16[1,128,4096]{2,1,0:T(8,128)(2,1)} %qr_hbm.1, bf16[1,256,512]{2,1,0:T(8,128)(2,1)} %cl_hbm.1, bf16[1,64,256]{2,1,0:T(8,128)(2,1)} %bitcast.1, bf16[1,32,512]{2,1,0:T(8,128)(2,1)} %nl_hbm.1, bf16[1,32,64]{2,1,0:T(8,128)(2,1)} %nr_hbm.1, ...), custom_call_target="tpu_custom_call" | custom-call | flops 7000000000 | bytes 7000000 | tf_op jit(solution)/shard_map/latent_attention/pallas_call | solution.py:251
  20.2 0.8 %copy.11 = bf16[1,128,2048]{2,1,0:T(8,128)(2,1)} copy(bf16[1,128,2048]{2,1,0:T(8,128)(2,1)S(1)} %latent_attention.1) | data formatting | bytes 1048576

commit v4 on v3

--- a/solution.py
+++ b/solution.py
@@ -30,15 +30,19 @@
 BF16 = jnp.bfloat16
 
 NEW0 = 2 * ROWS
-FIRST = NEW0 + CTX * NEW
-SECOND = FIRST + 2 * HALF
+FAR0 = NEW0 + CTX * NEW
 SLOT_ROWS = (
     ((0, 0, ROWS),),
     ((ROWS, 0, ROWS),),
-    ((FIRST, 0, HALF), (SECOND, HALF, HALF)),
-    ((FIRST + HALF, 0, HALF), (SECOND + HALF, HALF, HALF)),
+    ((FAR0, 0, HALF), (FAR0 + 2 * HALF, HALF, HALF)),
+    ((FAR0 + HALF, 0, HALF), (FAR0 + 3 * HALF, HALF, HALF)),
 )
-CHUNKS = ((0, 2 * ROWS), (NEW0, CTX * NEW + 2 * HALF), (SECOND, 2 * HALF))
+CHUNKS = (
+    (0, 2 * ROWS),
+    (NEW0, CTX * NEW + HALF),
+    (FAR0 + HALF, 2 * HALF),
+    (FAR0 + 3 * HALF, HALF),
+)
 
 
 def kernel(
@@ -69,7 +73,7 @@
     barrier = pltpu.get_barrier_semaphore()
     for peer in (sib, par):
         pl.semaphore_signal(barrier, inc=1, device_id={"ctx": peer}, device_id_type=MESH)
-    for name in ("wk", "qn", "qr", "cl", "cr", "nl", "nr", "ln", "wv"):
+    for name in ("wk", "qn", "qr", "cl", "cr", "nl", "nr", "ln"):
         loads[name].start()
     pl.semaphore_wait(barrier, 2)
 
@@ -104,6 +108,7 @@
     ]
     for copy in to_par + to_sib:
         copy.start()
+    loads["wv"].start()
 
     row_of = lax.broadcasted_iota(jnp.int32, (KEXT - DC - DR, 2 * Q), 0)
     tail = jnp.where(row_of == 0, BLOCKED, 0.0).astype(BF16)
@@ -189,6 +194,16 @@
         )
         acc[pair] = acc[pair] * factor[index % 2][...] + part if chunk else part
 
+    def finish(index):
+        pair = items[index][1]
+        mean = (acc[pair] * (1.0 / total[pair])).astype(BF16)
+        for side in range(2):
+            head = 2 * pair + side
+            out[0, :, head * DV : (head + 1) * DV] = lax.dot_general(
+                mean[:, side * Q : (side + 1) * Q], wv[:, head * DV : (head + 1) * DV],
+                (((0,), (0,)), ((), ())), preferred_element_type=F32,
+            ).astype(BF16)
+
     def onward(indices):
         for k in indices:
             to_par[k].wait_recv()
@@ -203,41 +218,49 @@
             for slot in range(2):
                 prepare_new(slot)
                 prepare_cached(slot)
-            turn(0, NEW0)
-        if index == 3:
+            turn(*CHUNKS[0])
+        if index == 5:
             onward(range(4))
         if index == PAIRS:
             onward(range(4, 5))
-            for copy in forward[:5]:
+            for copy in forward[:4]:
                 copy.wait_recv()
             for slot in range(2, 4):
                 prepare_new(slot)
                 prepare_cached(slot)
-            turn(NEW0, SECOND - NEW0)
-        if index == 2 * PAIRS - 3:
+            turn(*CHUNKS[1])
+        if index == 2 * PAIRS:
             onward(range(5, 6))
-        if index == 2 * PAIRS:
+            forward[4].wait_recv()
+            turn(*CHUNKS[2])
+        if index == 3 * PAIRS:
             forward[5].wait_recv()
-            turn(SECOND, NROW - SECOND)
-
-    for index in range(len(items) + 2):
-        if index < len(items):
-            before_item(index)
-            score_of(index)
-        if 1 <= index <= len(items):
-            weigh(index - 1)
+            loads["wv"].wait()
+            turn(*CHUNKS[3])
+
+    stages = (score_of, weigh, gather_in)
+    done = [0, 0, 0]
+
+    def advance(stage, index):
+        if done[stage] <= index < len(items):
+            assert done[stage] == index
+            done[stage] += 1
+            stages[stage](index)
+
+    last = len(items) - PAIRS
+    for index in range(len(items) + 3):
+        if index in (PAIRS, 2 * PAIRS):
+            advance(1, index - 1)
+            advance(2, index - 2)
+            advance(2, index - 1)
+        before_item(index)
+        advance(0, index)
+        if index >= 1:
+            advance(1, index - 1)
         if index >= 2:
-            gather_in(index - 2)
-
-    loads["wv"].wait()
-    for pair in range(PAIRS):
-        mean = (acc[pair] * (1.0 / total[pair])).astype(BF16)
-        for side in range(2):
-            head = 2 * pair + side
-            out[0, :, head * DV : (head + 1) * DV] = lax.dot_general(
-                mean[:, side * Q : (side + 1) * Q], wv[:, head * DV : (head + 1) * DV],
-                (((0,), (0,)), ((), ())), preferred_element_type=F32,
-            ).astype(BF16)
+            advance(2, index - 2)
+        if index >= last + 3:
+            finish(index - 3)
     for copy in to_par + to_sib + forward:
         copy.wait_send()
 

time: 21.1 us -> 19.2 us (0.910)
  Pallas kernels: 19.5 us -> 17.6 us
    pallas_call x1, Pallas kernels: 19.5 us -> 17.6 us  [shards(): pl.pallas_call(kernel, out_shape=pltpu.VMEM((1, Q, HERE * DV), BF16), in_...]
where the time goes in v4:
time: 19.2 us; the launch traced here: 19.1 us
  Pallas kernels  17.6 us (92%)
  local copies, waits for them, and re-layouts  0.8 us (4%)
  between operations  0.66 us (3%)
    pallas_call x1, Pallas kernels, shards(): pl.pallas_call(kernel, out_shape=pltpu.VMEM((1, Q, HERE * DV), BF16), in_...  17.6 us
    unnamed x1, local copies, waits for them, and re-layouts  0.8 us

profile of v4, /device:TPU:1, one launch (start us, length us, event | category | flops | bytes accessed | tf_op | source)
XLA Modules:
  0.0 19.1 jit_solution(14725574767381625175)
XLA Ops:
  0.7 17.6 %latent_attention.1 = bf16[1,128,2048]{2,1,0:T(8,128)(2,1)S(1)} custom-call(bf16[1,128,8192]{2,1,0:T(8,128)(2,1)} %qn_hbm.1, bf16[1,128,4096]{2,1,0:T(8,128)(2,1)} %qr_hbm.1, bf16[1,256,512]{2,1,0:T(8,128)(2,1)} %cl_hbm.1, bf16[1,64,256]{2,1,0:T(8,128)(2,1)} %bitcast.1, bf16[1,32,512]{2,1,0:T(8,128)(2,1)} %nl_hbm.1, bf16[1,32,64]{2,1,0:T(8,128)(2,1)} %nr_hbm.1, ...), custom_call_target="tpu_custom_call" | custom-call | flops 7000000000 | bytes 7000000 | tf_op jit(solution)/shard_map/latent_attention/pallas_call | solution.py:274
  18.3 0.8 %copy.11 = bf16[1,128,2048]{2,1,0:T(8,128)(2,1)} copy(bf16[1,128,2048]{2,1,0:T(8,128)(2,1)S(1)} %latent_attention.1) | data formatting | bytes 1048576

commit v5 on v4

--- a/solution.py
+++ b/solution.py
@@ -19,7 +19,6 @@
 Q = 128
 ROWS = 256
 NEW = 32
-HALF = ROWS // 2
 NROW = CTX * (ROWS + NEW)
 KEXT = DC + 128
 LOG2E = 1.4426950408889634
@@ -29,27 +28,37 @@
 F32 = jnp.float32
 BF16 = jnp.bfloat16
 
+PIECES = (128, 80, 48)
+STARTS = (0, 128, 208)
+RELAYED = 2
 NEW0 = 2 * ROWS
 FAR0 = NEW0 + CTX * NEW
+LANDS = (
+    None,
+    (ROWS,),
+    (FAR0, FAR0 + 2 * PIECES[0], FAR0 + 2 * PIECES[0] + 2 * PIECES[1]),
+    (FAR0 + PIECES[0], FAR0 + 2 * PIECES[0] + PIECES[1], FAR0 + 2 * PIECES[0] + 2 * PIECES[1] + PIECES[2]),
+)
 SLOT_ROWS = (
     ((0, 0, ROWS),),
     ((ROWS, 0, ROWS),),
-    ((FAR0, 0, HALF), (FAR0 + 2 * HALF, HALF, HALF)),
-    ((FAR0 + HALF, 0, HALF), (FAR0 + 3 * HALF, HALF, HALF)),
+    tuple(zip(LANDS[2], STARTS, PIECES)),
+    tuple(zip(LANDS[3], STARTS, PIECES)),
 )
 CHUNKS = (
-    (0, 2 * ROWS),
-    (NEW0, CTX * NEW + HALF),
-    (FAR0 + HALF, 2 * HALF),
-    (FAR0 + 3 * HALF, HALF),
+    (0, 2 * ROWS, 0, 2 * ROWS),
+    (NEW0, CTX * NEW + PIECES[0], 512, 256),
+    (LANDS[3][0], PIECES[0] + PIECES[1], 768, 256),
+    (LANDS[3][1], PIECES[1] + 2 * PIECES[2], 1024, 256),
 )
+TURNED = 1280
 
 
 def kernel(
     qn_hbm, qr_hbm, cl_hbm, cr_hbm, nl_hbm, nr_hbm, len_hbm, wk_hbm, wv_hbm, out,
     qn, qr, wk, wv, lat, rope, nrope, lens, ext, latt, qt, acc, top, total,
     score0, score1, weight0, weight1, factor0, factor1,
-    load_sem, sib_send, sib_recv, par_send, par_recv, fwd_send, fwd_recv,
+    load_sem, sib_send, sib_recv, par_send, par_recv, fwd_send, fwd_recv, far_send, far_recv,
 ):
     me = lax.axis_index("ctx")
     sib = me + 1 - 2 * lax.rem(me, 2)
@@ -71,11 +80,11 @@
         wv=local(8, wv_hbm, wv),
     )
     barrier = pltpu.get_barrier_semaphore()
-    for peer in (sib, par):
+    for peer in (sib, par, far):
         pl.semaphore_signal(barrier, inc=1, device_id={"ctx": peer}, device_id_type=MESH)
     for name in ("wk", "qn", "qr", "cl", "cr", "nl", "nr", "ln"):
         loads[name].start()
-    pl.semaphore_wait(barrier, 2)
+    pl.semaphore_wait(barrier, 3)
 
     def remote(src, dst, send, recv, index, peer):
         return pltpu.make_async_remote_copy(
@@ -89,14 +98,14 @@
         )
 
     mine = (nr_hbm.at[0], nl_hbm.at[0], len_hbm, cr_hbm.at[0])
-    halves = tuple(cl_hbm.at[0, pl.ds(HALF * k, HALF)] for k in range(2))
+    pieces = tuple(cl_hbm.at[0, pl.ds(start, count)] for start, count in zip(STARTS, PIECES))
 
     def landed(slot):
         return tuple(lat.at[pl.ds(row, count)] for row, _, count in SLOT_ROWS[slot])
 
     to_par = [
         remote(src, dst, par_send, par_recv, k, par)
-        for k, (src, dst) in enumerate(zip(mine + halves, small(2) + landed(2)))
+        for k, (src, dst) in enumerate(zip(mine + pieces, small(2) + landed(2)))
     ]
     to_sib = [
         remote(src, dst, sib_send, sib_recv, k, sib)
@@ -104,9 +113,10 @@
     ]
     forward = [
         remote(src, dst, fwd_send, fwd_recv, k, sib)
-        for k, (src, dst) in enumerate(zip(small(2) + landed(2), small(3) + landed(3)))
+        for k, (src, dst) in enumerate(zip(small(2) + landed(2)[:RELAYED], small(3) + landed(3)[:RELAYED]))
     ]
-    for copy in to_par + to_sib:
+    to_far = remote(pieces[RELAYED], landed(3)[RELAYED], far_send, far_recv, 0, far)
+    for copy in to_par[:4] + to_sib + to_par[4:] + [to_far]:
         copy.start()
     loads["wv"].start()
 
@@ -146,8 +156,11 @@
         for begin, first, count in SLOT_ROWS[slot]:
             ext[begin : begin + count, :] = wide[first : first + count]
 
-    def turn(begin, count):
-        latt[:, begin : begin + count] = lat[begin : begin + count, :].T
+    def turn(begin, count, column, columns):
+        rows = lat[begin : begin + count, :]
+        if columns > count:
+            rows = jnp.concatenate([rows, jnp.zeros((columns - count, DC), BF16)], axis=0)
+        latt[:, column : column + columns] = rows.T
 
     local_row = lax.broadcasted_iota(jnp.int32, (CTX * NEW, 2 * Q), 0)
     query = lax.rem(lax.broadcasted_iota(jnp.int32, (CTX * NEW, 2 * Q), 1), Q)
@@ -162,7 +175,7 @@
 
     def score_of(index):
         chunk, pair = items[index]
-        begin, count = CHUNKS[chunk]
+        begin, count = CHUNKS[chunk][:2]
         keys = jnp.concatenate(
             [lat[begin : begin + count, :], ext[begin : begin + count, :]], axis=1
         )
@@ -170,7 +183,7 @@
 
     def weigh(index):
         chunk, pair = items[index]
-        begin, count = CHUNKS[chunk]
+        begin, count, _, columns = CHUNKS[chunk]
         scores = score[index % 2][:count]
         if begin == NEW0:
             new = CTX * NEW
@@ -184,13 +197,18 @@
         sums = jnp.sum(weights, axis=0, keepdims=True)
         top[pair] = level
         total[pair] = total[pair] * change + sums if chunk else sums
-        weight[index % 2][:count] = weights.astype(BF16)
+        weights = weights.astype(BF16)
+        if columns > count:
+            weights = jnp.concatenate([weights, jnp.zeros((columns - count, 2 * Q), BF16)], axis=0)
+        weight[index % 2][:columns] = weights
 
     def gather_in(index):
         chunk, pair = items[index]
-        begin, count = CHUNKS[chunk]
+        _, _, column, columns = CHUNKS[chunk]
         part = jnp.dot(
-            latt[:, begin : begin + count], weight[index % 2][:count], preferred_element_type=F32
+            latt[:, column : column + columns],
+            weight[index % 2][:columns],
+            preferred_element_type=F32,
         )
         acc[pair] = acc[pair] * factor[index % 2][...] + part if chunk else part
 
@@ -234,8 +252,10 @@
             forward[4].wait_recv()
             turn(*CHUNKS[2])
         if index == 3 * PAIRS:
+            loads["wv"].wait()
             forward[5].wait_recv()
-            loads["wv"].wait()
+            to_par[6].wait_recv()
+            to_far.wait_recv()
             turn(*CHUNKS[3])
 
     stages = (score_of, weigh, gather_in)
@@ -261,7 +281,7 @@
             advance(2, index - 2)
         if index >= last + 3:
             finish(index - 3)
-    for copy in to_par + to_sib + forward:
+    for copy in to_par + to_sib + forward + [to_far]:
         copy.wait_send()
 
 
@@ -286,7 +306,7 @@
             pltpu.VMEM((CTX, NEW, DR), BF16),
             pltpu.VMEM((CTX, 1, 1), jnp.int32),
             pltpu.VMEM((NROW, KEXT - DC), BF16),
-            pltpu.VMEM((DC, NROW), BF16),
+            pltpu.VMEM((DC, TURNED), BF16),
             pltpu.VMEM((PAIRS, KEXT, 2 * Q), BF16),
             pltpu.VMEM((PAIRS, DC, 2 * Q), F32),
             pltpu.VMEM((PAIRS, 1, 2 * Q), F32),
@@ -299,7 +319,8 @@
             pltpu.VMEM((1, 2 * Q), F32),
             pltpu.SemaphoreType.DMA((9,)),
         ]
-        + [pltpu.SemaphoreType.DMA((6,))] * 6,
+        + [pltpu.SemaphoreType.DMA((7,))] * 6
+        + [pltpu.SemaphoreType.DMA((1,))] * 2,
         compiler_params=pltpu.CompilerParams(
             collective_id=0, has_side_effects=True, vmem_limit_bytes=40 << 20
         ),

time: 19.2 us -> 20.2 us (1.052)
  Pallas kernels: 17.6 us -> 18.7 us
    pallas_call x1, Pallas kernels: 17.6 us -> 18.7 us  [shards(): pl.pallas_call(kernel, out_shape=pltpu.VMEM((1, Q, HERE * DV), BF16), in_...]
where the time goes in v5:
time: 20.2 us; the launch traced here: 20.1 us
  Pallas kernels  18.7 us (93%)
  local copies, waits for them, and re-layouts  0.8 us (4%)
  between operations  0.66 us (3%)
    pallas_call x1, Pallas kernels, shards(): pl.pallas_call(kernel, out_shape=pltpu.VMEM((1, Q, HERE * DV), BF16), in_...  18.7 us
    unnamed x1, local copies, waits for them, and re-layouts  0.8 us

profile of v5, /device:TPU:1, one launch (start us, length us, event | category | flops | bytes accessed | tf_op | source)
XLA Modules:
  0.0 20.1 jit_solution(7004157030821104766)
XLA Ops:
  0.7 18.7 %latent_attention.1 = bf16[1,128,2048]{2,1,0:T(8,128)(2,1)S(1)} custom-call(bf16[1,128,8192]{2,1,0:T(8,128)(2,1)} %qn_hbm.1, bf16[1,128,4096]{2,1,0:T(8,128)(2,1)} %qr_hbm.1, bf16[1,256,512]{2,1,0:T(8,128)(2,1)} %cl_hbm.1, bf16[1,64,256]{2,1,0:T(8,128)(2,1)} %bitcast.1, bf16[1,32,512]{2,1,0:T(8,128)(2,1)} %nl_hbm.1, bf16[1,32,64]{2,1,0:T(8,128)(2,1)} %nr_hbm.1, ...), custom_call_target="tpu_custom_call" | custom-call | flops 7000000000 | bytes 7000000 | tf_op jit(solution)/shard_map/latent_attention/pallas_call | solution.py:294
  19.3 0.8 %copy.11 = bf16[1,128,2048]{2,1,0:T(8,128)(2,1)} copy(bf16[1,128,2048]{2,1,0:T(8,128)(2,1)S(1)} %latent_attention.1) | data formatting | bytes 1048576

commit v6 on v5

--- a/solution.py
+++ b/solution.py
@@ -116,7 +116,7 @@
         for k, (src, dst) in enumerate(zip(small(2) + landed(2)[:RELAYED], small(3) + landed(3)[:RELAYED]))
     ]
     to_far = remote(pieces[RELAYED], landed(3)[RELAYED], far_send, far_recv, 0, far)
-    for copy in to_par[:4] + to_sib + to_par[4:] + [to_far]:
+    for copy in to_par[:5] + to_sib:
         copy.start()
     loads["wv"].start()
 
@@ -237,9 +237,13 @@
                 prepare_new(slot)
                 prepare_cached(slot)
             turn(*CHUNKS[0])
-        if index == 5:
+        if index == PAIRS - 2:
+            to_par[5].start()
+        if index == PAIRS:
             onward(range(4))
-        if index == PAIRS:
+            to_par[5].wait_send()
+            to_par[6].start()
+            to_far.start()
             onward(range(4, 5))
             for copy in forward[:4]:
                 copy.wait_recv()
@@ -269,7 +273,7 @@
 
     last = len(items) - PAIRS
     for index in range(len(items) + 3):
-        if index in (PAIRS, 2 * PAIRS):
+        if index in (PAIRS, 2 * PAIRS, 3 * PAIRS):
             advance(1, index - 1)
             advance(2, index - 2)
             advance(2, index - 1)
@@ -281,7 +285,7 @@
             advance(2, index - 2)
         if index >= last + 3:
             finish(index - 3)
-    for copy in to_par + to_sib + forward + [to_far]:
+    for copy in to_par[:5] + to_par[6:] + to_sib + forward + [to_far]:
         copy.wait_send()
 
 

time: 20.2 us -> 20.3 us (level)
  no operation moved by 1% of the time
where the time goes in v6:
time: 20.3 us; the launch traced here: 20.2 us
  Pallas kernels  18.7 us (92%)
  local copies, waits for them, and re-layouts  0.8 us (4%)
  between operations  0.66 us (3%)
    pallas_call x1, Pallas kernels, shards(): pl.pallas_call(kernel, out_shape=pltpu.VMEM((1, Q, HERE * DV), BF16), in_...  18.7 us
    unnamed x1, local copies, waits for them, and re-layouts  0.8 us

profile of v6, /device:TPU:1, one launch (start us, length us, event | category | flops | bytes accessed | tf_op | source)
XLA Modules:
  0.0 20.2 jit_solution(17290896241311664918)
XLA Ops:
  0.7 18.7 %latent_attention.1 = bf16[1,128,2048]{2,1,0:T(8,128)(2,1)S(1)} custom-call(bf16[1,128,8192]{2,1,0:T(8,128)(2,1)} %qn_hbm.1, bf16[1,128,4096]{2,1,0:T(8,128)(2,1)} %qr_hbm.1, bf16[1,256,512]{2,1,0:T(8,128)(2,1)} %cl_hbm.1, bf16[1,64,256]{2,1,0:T(8,128)(2,1)} %bitcast.1, bf16[1,32,512]{2,1,0:T(8,128)(2,1)} %nl_hbm.1, bf16[1,32,64]{2,1,0:T(8,128)(2,1)} %nr_hbm.1, ...), custom_call_target="tpu_custom_call" | custom-call | flops 7000000000 | bytes 7000000 | tf_op jit(solution)/shard_map/latent_attention/pallas_call | solution.py:298
  19.4 0.8 %copy.11 = bf16[1,128,2048]{2,1,0:T(8,128)(2,1)} copy(bf16[1,128,2048]{2,1,0:T(8,128)(2,1)S(1)} %latent_attention.1) | data formatting | bytes 1048576

commit v7 on v5

--- a/solution.py
+++ b/solution.py
@@ -31,13 +31,15 @@
 PIECES = (128, 80, 48)
 STARTS = (0, 128, 208)
 RELAYED = 2
-NEW0 = 2 * ROWS
-FAR0 = NEW0 + CTX * NEW
+NEAR0 = 2 * ROWS
+FAR0 = NEAR0 + 3 * NEW + PIECES[0]
+LAST0 = FAR0 + NEW + PIECES[0] + PIECES[1]
+NEWS = (NEAR0, NEAR0 + NEW, NEAR0 + 2 * NEW, FAR0)
 LANDS = (
     None,
     (ROWS,),
-    (FAR0, FAR0 + 2 * PIECES[0], FAR0 + 2 * PIECES[0] + 2 * PIECES[1]),
-    (FAR0 + PIECES[0], FAR0 + 2 * PIECES[0] + PIECES[1], FAR0 + 2 * PIECES[0] + 2 * PIECES[1] + PIECES[2]),
+    (NEAR0 + 3 * NEW, LAST0 - PIECES[1], LAST0 + PIECES[1]),
+    (FAR0 + NEW, LAST0, LAST0 + PIECES[1] + PIECES[2]),
 )
 SLOT_ROWS = (
     ((0, 0, ROWS),),
@@ -46,10 +48,11 @@
     tuple(zip(LANDS[3], STARTS, PIECES)),
 )
 CHUNKS = (
-    (0, 2 * ROWS, 0, 2 * ROWS),
-    (NEW0, CTX * NEW + PIECES[0], 512, 256),
-    (LANDS[3][0], PIECES[0] + PIECES[1], 768, 256),
-    (LANDS[3][1], PIECES[1] + 2 * PIECES[2], 1024, 256),
+    (0, ROWS, 0, ROWS),
+    (ROWS, ROWS, ROWS, ROWS),
+    (NEAR0, FAR0 - NEAR0, 512, 256),
+    (FAR0, LAST0 - FAR0, 768, 256),
+    (LAST0, NROW - LAST0, 1024, 256),
 )
 TURNED = 1280
 
@@ -74,7 +77,7 @@
         qr=local(2, qr_hbm.at[0, :, pl.ds(pl.multiple_of(me * HERE * DR, HERE * DR), HERE * DR)], qr),
         cl=local(3, cl_hbm.at[0], lat.at[pl.ds(0, ROWS)]),
         cr=local(4, cr_hbm.at[0], rope.at[0]),
-        nl=local(5, nl_hbm.at[0], lat.at[pl.ds(NEW0, NEW)]),
+        nl=local(5, nl_hbm.at[0], lat.at[pl.ds(NEWS[0], NEW)]),
         nr=local(6, nr_hbm.at[0], nrope.at[0]),
         ln=local(7, len_hbm, lens.at[0]),
         wv=local(8, wv_hbm, wv),
@@ -94,7 +97,7 @@
 
     def small(slot):
         return (
-            nrope.at[slot], lat.at[pl.ds(NEW0 + slot * NEW, NEW)], lens.at[slot], rope.at[slot],
+            nrope.at[slot], lat.at[pl.ds(NEWS[slot], NEW)], lens.at[slot], rope.at[slot],
         )
 
     mine = (nr_hbm.at[0], nl_hbm.at[0], len_hbm, cr_hbm.at[0])
@@ -116,9 +119,8 @@
         for k, (src, dst) in enumerate(zip(small(2) + landed(2)[:RELAYED], small(3) + landed(3)[:RELAYED]))
     ]
     to_far = remote(pieces[RELAYED], landed(3)[RELAYED], far_send, far_recv, 0, far)
-    for copy in to_par[:4] + to_sib + to_par[4:] + [to_far]:
+    for copy in to_par[:4] + to_sib:
         copy.start()
-    loads["wv"].start()
 
     row_of = lax.broadcasted_iota(jnp.int32, (KEXT - DC - DR, 2 * Q), 0)
     tail = jnp.where(row_of == 0, BLOCKED, 0.0).astype(BF16)
@@ -128,6 +130,8 @@
     loads["wk"].wait()
     loads["qn"].wait()
     loads["qr"].wait()
+    to_par[4].start()
+    loads["wv"].start()
     for head in range(HERE):
         pair, side = head // 2, (head % 2) * Q
         part = lax.dot_general(
@@ -144,7 +148,7 @@
     row = lax.broadcasted_iota(jnp.int32, (DR, ROWS), 0)
 
     def prepare_new(slot):
-        begin = NEW0 + slot * NEW
+        begin = NEWS[slot]
         ext[begin : begin + NEW, :] = jnp.concatenate(
             [nrope[slot], jnp.zeros((NEW, KEXT - DC - DR), BF16)], axis=1
         )
@@ -185,9 +189,10 @@
         chunk, pair = items[index]
         begin, count, _, columns = CHUNKS[chunk]
         scores = score[index % 2][:count]
-        if begin == NEW0:
-            new = CTX * NEW
-            scores = jnp.concatenate([jnp.where(fresh, scores[:new], BLOCKED), scores[new:]], axis=0)
+        if begin in (NEAR0, FAR0):
+            new = 3 * NEW if begin == NEAR0 else NEW
+            seen = fresh[: 3 * NEW] if begin == NEAR0 else fresh[3 * NEW :]
+            scores = jnp.concatenate([jnp.where(seen, scores[:new], BLOCKED), scores[new:]], axis=0)
         level = jnp.max(scores, axis=0, keepdims=True)
         if chunk:
             level = jnp.maximum(top[pair], level)
@@ -231,32 +236,40 @@
         if index == 0:
             for name in ("cl", "cr", "nl", "nr", "ln"):
                 loads[name].wait()
+            prepare_new(0)
+            prepare_cached(0)
+            turn(*CHUNKS[0])
+        if index == PAIRS - 1:
+            to_par[5].start()
+        if index == PAIRS:
             for copy in to_sib:
                 copy.wait_recv()
-            for slot in range(2):
-                prepare_new(slot)
-                prepare_cached(slot)
-            turn(*CHUNKS[0])
-        if index == 5:
+            prepare_new(1)
+            prepare_cached(1)
+            turn(*CHUNKS[1])
+        if index == 2 * PAIRS - 3:
+            to_par[6].start()
+            to_far.start()
+        if index == 2 * PAIRS - 1:
             onward(range(4))
-        if index == PAIRS:
+        if index == 2 * PAIRS:
             onward(range(4, 5))
-            for copy in forward[:4]:
-                copy.wait_recv()
-            for slot in range(2, 4):
-                prepare_new(slot)
-                prepare_cached(slot)
-            turn(*CHUNKS[1])
-        if index == 2 * PAIRS:
-            onward(range(5, 6))
-            forward[4].wait_recv()
+            prepare_new(2)
+            prepare_cached(2)
             turn(*CHUNKS[2])
         if index == 3 * PAIRS:
+            onward(range(5, 6))
+            for copy in forward[:5]:
+                copy.wait_recv()
+            prepare_new(3)
+            prepare_cached(3)
+            turn(*CHUNKS[3])
+        if index == 4 * PAIRS:
             loads["wv"].wait()
             forward[5].wait_recv()
             to_par[6].wait_recv()
             to_far.wait_recv()
-            turn(*CHUNKS[3])
+            turn(*CHUNKS[4])
 
     stages = (score_of, weigh, gather_in)
     done = [0, 0, 0]
@@ -269,7 +282,7 @@
 
     last = len(items) - PAIRS
     for index in range(len(items) + 3):
-        if index in (PAIRS, 2 * PAIRS):
+        if index in (2 * PAIRS, 3 * PAIRS, 4 * PAIRS):
             advance(1, index - 1)
             advance(2, index - 2)
             advance(2, index - 1)

time: 20.2 us -> 20.1 us (level)
  no operation moved by 1% of the time
where the time goes in v7:
time: 20.1 us; the launch traced here: 20 us
  Pallas kernels  18.6 us (93%)
  local copies, waits for them, and re-layouts  0.8 us (4%)
  between operations  0.66 us (3%)
    pallas_call x1, Pallas kernels, shards(): pl.pallas_call(kernel, out_shape=pltpu.VMEM((1, Q, HERE * DV), BF16), in_...  18.6 us
    unnamed x1, local copies, waits for them, and re-layouts  0.8 us

profile of v7, /device:TPU:1, one launch (start us, length us, event | category | flops | bytes accessed | tf_op | source)
XLA Modules:
  0.0 20.0 jit_solution(11368905216753213811)
XLA Ops:
  0.7 18.6 %latent_attention.1 = bf16[1,128,2048]{2,1,0:T(8,128)(2,1)S(1)} custom-call(bf16[1,128,8192]{2,1,0:T(8,128)(2,1)} %qn_hbm.1, bf16[1,128,4096]{2,1,0:T(8,128)(2,1)} %qr_hbm.1, bf16[1,256,512]{2,1,0:T(8,128)(2,1)} %cl_hbm.1, bf16[1,64,256]{2,1,0:T(8,128)(2,1)} %bitcast.1, bf16[1,32,512]{2,1,0:T(8,128)(2,1)} %nl_hbm.1, bf16[1,32,64]{2,1,0:T(8,128)(2,1)} %nr_hbm.1, ...), custom_call_target="tpu_custom_call" | custom-call | flops 7000000000 | bytes 7000000 | tf_op jit(solution)/shard_map/latent_attention/pallas_call | solution.py:307
  19.2 0.8 %copy.11 = bf16[1,128,2048]{2,1,0:T(8,128)(2,1)} copy(bf16[1,128,2048]{2,1,0:T(8,128)(2,1)S(1)} %latent_attention.1) | data formatting | bytes 1048576

commit v8 on v7

--- a/solution.py
+++ b/solution.py
@@ -32,15 +32,16 @@
 STARTS = (0, 128, 208)
 RELAYED = 2
 NEAR0 = 2 * ROWS
-FAR0 = NEAR0 + 3 * NEW + PIECES[0]
+FAR0 = NEAR0 + 2 * NEW + PIECES[0]
 LAST0 = FAR0 + NEW + PIECES[0] + PIECES[1]
-NEWS = (NEAR0, NEAR0 + NEW, NEAR0 + 2 * NEW, FAR0)
+NEWS = (NEAR0, NEAR0 + NEW, FAR0, LAST0)
 LANDS = (
     None,
     (ROWS,),
-    (NEAR0 + 3 * NEW, LAST0 - PIECES[1], LAST0 + PIECES[1]),
-    (FAR0 + NEW, LAST0, LAST0 + PIECES[1] + PIECES[2]),
+    (NEAR0 + 2 * NEW, LAST0 - PIECES[1], LAST0 + NEW + PIECES[1]),
+    (FAR0 + NEW, LAST0 + NEW, LAST0 + NEW + PIECES[1] + PIECES[2]),
 )
+FRESH = {NEAR0: (0, 2 * NEW), FAR0: (2 * NEW, 3 * NEW), LAST0: (3 * NEW, 4 * NEW)}
 SLOT_ROWS = (
     ((0, 0, ROWS),),
     ((ROWS, 0, ROWS),),
@@ -61,7 +62,7 @@
     qn_hbm, qr_hbm, cl_hbm, cr_hbm, nl_hbm, nr_hbm, len_hbm, wk_hbm, wv_hbm, out,
     qn, qr, wk, wv, lat, rope, nrope, lens, ext, latt, qt, acc, top, total,
     score0, score1, weight0, weight1, factor0, factor1,
-    load_sem, sib_send, sib_recv, par_send, par_recv, fwd_send, fwd_recv, far_send, far_recv,
+    load_sem, sib_send, sib_recv, par_send, par_recv, fwd_send, fwd_recv, far_send, far_recv, ready,
 ):
     me = lax.axis_index("ctx")
     sib = me + 1 - 2 * lax.rem(me, 2)
@@ -83,11 +84,12 @@
         wv=local(8, wv_hbm, wv),
     )
     barrier = pltpu.get_barrier_semaphore()
-    for peer in (sib, par, far):
+    for peer in (sib, par):
         pl.semaphore_signal(barrier, inc=1, device_id={"ctx": peer}, device_id_type=MESH)
     for name in ("wk", "qn", "qr", "cl", "cr", "nl", "nr", "ln"):
         loads[name].start()
-    pl.semaphore_wait(barrier, 3)
+    pl.semaphore_wait(barrier, 2)
+    pl.semaphore_signal(ready, inc=1, device_id={"ctx": sib}, device_id_type=MESH)
 
     def remote(src, dst, send, recv, index, peer):
         return pltpu.make_async_remote_copy(
@@ -97,10 +99,10 @@
 
     def small(slot):
         return (
-            nrope.at[slot], lat.at[pl.ds(NEWS[slot], NEW)], lens.at[slot], rope.at[slot],
-        )
-
-    mine = (nr_hbm.at[0], nl_hbm.at[0], len_hbm, cr_hbm.at[0])
+            rope.at[slot], lens.at[slot], nrope.at[slot], lat.at[pl.ds(NEWS[slot], NEW)],
+        )
+
+    mine = (cr_hbm.at[0], len_hbm, nr_hbm.at[0], nl_hbm.at[0])
     pieces = tuple(cl_hbm.at[0, pl.ds(start, count)] for start, count in zip(STARTS, PIECES))
 
     def landed(slot):
@@ -119,7 +121,7 @@
         for k, (src, dst) in enumerate(zip(small(2) + landed(2)[:RELAYED], small(3) + landed(3)[:RELAYED]))
     ]
     to_far = remote(pieces[RELAYED], landed(3)[RELAYED], far_send, far_recv, 0, far)
-    for copy in to_par[:4] + to_sib:
+    for copy in to_par[:2] + to_par[4:5] + to_sib:
         copy.start()
 
     row_of = lax.broadcasted_iota(jnp.int32, (KEXT - DC - DR, 2 * Q), 0)
@@ -130,7 +132,6 @@
     loads["wk"].wait()
     loads["qn"].wait()
     loads["qr"].wait()
-    to_par[4].start()
     loads["wv"].start()
     for head in range(HERE):
         pair, side = head // 2, (head % 2) * Q
@@ -189,10 +190,12 @@
         chunk, pair = items[index]
         begin, count, _, columns = CHUNKS[chunk]
         scores = score[index % 2][:count]
-        if begin in (NEAR0, FAR0):
-            new = 3 * NEW if begin == NEAR0 else NEW
-            seen = fresh[: 3 * NEW] if begin == NEAR0 else fresh[3 * NEW :]
-            scores = jnp.concatenate([jnp.where(seen, scores[:new], BLOCKED), scores[new:]], axis=0)
+        if begin in FRESH:
+            lo, hi = FRESH[begin]
+            new = hi - lo
+            scores = jnp.concatenate(
+                [jnp.where(fresh[lo:hi], scores[:new], BLOCKED), scores[new:]], axis=0
+            )
         level = jnp.max(scores, axis=0, keepdims=True)
         if chunk:
             level = jnp.maximum(top[pair], level)
@@ -240,35 +243,37 @@
             prepare_cached(0)
             turn(*CHUNKS[0])
         if index == PAIRS - 1:
-            to_par[5].start()
+            for k in (2, 3, 5):
+                to_par[k].start()
         if index == PAIRS:
             for copy in to_sib:
                 copy.wait_recv()
             prepare_new(1)
             prepare_cached(1)
             turn(*CHUNKS[1])
-        if index == 2 * PAIRS - 3:
+        if index == 2 * PAIRS - 1:
+            pl.semaphore_wait(ready, 1)
             to_par[6].start()
             to_far.start()
-        if index == 2 * PAIRS - 1:
-            onward(range(4))
+            onward(range(2))
         if index == 2 * PAIRS:
             onward(range(4, 5))
-            prepare_new(2)
             prepare_cached(2)
             turn(*CHUNKS[2])
         if index == 3 * PAIRS:
-            onward(range(5, 6))
-            for copy in forward[:5]:
-                copy.wait_recv()
-            prepare_new(3)
+            onward((2, 3, 5))
+            for k in (0, 1, 4):
+                forward[k].wait_recv()
+            prepare_new(2)
             prepare_cached(3)
             turn(*CHUNKS[3])
         if index == 4 * PAIRS:
             loads["wv"].wait()
-            forward[5].wait_recv()
+            for k in (2, 3, 5):
+                forward[k].wait_recv()
             to_par[6].wait_recv()
             to_far.wait_recv()
+            prepare_new(3)
             turn(*CHUNKS[4])
 
     stages = (score_of, weigh, gather_in)
@@ -282,7 +287,7 @@
 
     last = len(items) - PAIRS
     for index in range(len(items) + 3):
-        if index in (2 * PAIRS, 3 * PAIRS, 4 * PAIRS):
+        if index in (2 * PAIRS, 3 * PAIRS):
             advance(1, index - 1)
             advance(2, index - 2)
             advance(2, index - 1)
@@ -333,7 +338,8 @@
             pltpu.SemaphoreType.DMA((9,)),
         ]
         + [pltpu.SemaphoreType.DMA((7,))] * 6
-        + [pltpu.SemaphoreType.DMA((1,))] * 2,
+        + [pltpu.SemaphoreType.DMA((1,))] * 2
+        + [pltpu.SemaphoreType.REGULAR],
         compiler_params=pltpu.CompilerParams(
             collective_id=0, has_side_effects=True, vmem_limit_bytes=40 << 20
         ),

time: 20.1 us -> 19.2 us (0.955)
  Pallas kernels: 18.6 us -> 17.7 us
    pallas_call x1, Pallas kernels: 18.6 us -> 17.7 us  [shards(): pl.pallas_call(kernel, out_shape=pltpu.VMEM((1, Q, HERE * DV), BF16), in_...]
where the time goes in v8:
time: 19.2 us; the launch traced here: 19.1 us
  Pallas kernels  17.7 us (92%)
  local copies, waits for them, and re-layouts  0.8 us (4%)
  between operations  0.66 us (3%)
    pallas_call x1, Pallas kernels, shards(): pl.pallas_call(kernel, out_shape=pltpu.VMEM((1, Q, HERE * DV), BF16), in_...  17.7 us
    unnamed x1, local copies, waits for them, and re-layouts  0.8 us

profile of v8, /device:TPU:1, one launch (start us, length us, event | category | flops | bytes accessed | tf_op | source)
XLA Modules:
  0.0 19.1 jit_solution(2246781392148713006)
XLA Ops:
  0.7 17.7 %latent_attention.1 = bf16[1,128,2048]{2,1,0:T(8,128)(2,1)S(1)} custom-call(bf16[1,128,8192]{2,1,0:T(8,128)(2,1)} %qn_hbm.1, bf16[1,128,4096]{2,1,0:T(8,128)(2,1)} %qr_hbm.1, bf16[1,256,512]{2,1,0:T(8,128)(2,1)} %cl_hbm.1, bf16[1,64,256]{2,1,0:T(8,128)(2,1)} %bitcast.1, bf16[1,32,512]{2,1,0:T(8,128)(2,1)} %nl_hbm.1, bf16[1,32,64]{2,1,0:T(8,128)(2,1)} %nr_hbm.1, ...), custom_call_target="tpu_custom_call" | custom-call | flops 7000000000 | bytes 7000000 | tf_op jit(solution)/shard_map/latent_attention/pallas_call | solution.py:312
  18.3 0.8 %copy.11 = bf16[1,128,2048]{2,1,0:T(8,128)(2,1)} copy(bf16[1,128,2048]{2,1,0:T(8,128)(2,1)S(1)} %latent_attention.1) | data formatting | bytes 1048576

commit v9 on v8

--- a/solution.py
+++ b/solution.py
@@ -252,14 +252,15 @@
             prepare_cached(1)
             turn(*CHUNKS[1])
         if index == 2 * PAIRS - 1:
-            pl.semaphore_wait(ready, 1)
-            to_par[6].start()
-            to_far.start()
             onward(range(2))
         if index == 2 * PAIRS:
             onward(range(4, 5))
             prepare_cached(2)
             turn(*CHUNKS[2])
+        if index == 2 * PAIRS + 2:
+            pl.semaphore_wait(ready, 1)
+            to_par[6].start()
+            to_far.start()
         if index == 3 * PAIRS:
             onward((2, 3, 5))
             for k in (0, 1, 4):
@@ -287,7 +288,7 @@
 
     last = len(items) - PAIRS
     for index in range(len(items) + 3):
-        if index in (2 * PAIRS, 3 * PAIRS):
+        if index in (2 * PAIRS, 3 * PAIRS, 4 * PAIRS):
             advance(1, index - 1)
             advance(2, index - 2)
             advance(2, index - 1)

time: 19.2 us -> 20.4 us (1.062)
  Pallas kernels: 17.7 us -> 18.9 us
    pallas_call x1, Pallas kernels: 17.7 us -> 18.9 us  [shards(): pl.pallas_call(kernel, out_shape=pltpu.VMEM((1, Q, HERE * DV), BF16), in_...]
where the time goes in v9:
time: 20.4 us; the launch traced here: 20.3 us
  Pallas kernels  18.9 us (93%)
  local copies, waits for them, and re-layouts  0.8 us (4%)
  between operations  0.66 us (3%)
    pallas_call x1, Pallas kernels, shards(): pl.pallas_call(kernel, out_shape=pltpu.VMEM((1, Q, HERE * DV), BF16), in_...  18.9 us
    unnamed x1, local copies, waits for them, and re-layouts  0.8 us

profile of v9, /device:TPU:1, one launch (start us, length us, event | category | flops | bytes accessed | tf_op | source)
XLA Modules:
  0.0 20.3 jit_solution(9321373592592575455)
XLA Ops:
  0.7 18.9 %latent_attention.1 = bf16[1,128,2048]{2,1,0:T(8,128)(2,1)S(1)} custom-call(bf16[1,128,8192]{2,1,0:T(8,128)(2,1)} %qn_hbm.1, bf16[1,128,4096]{2,1,0:T(8,128)(2,1)} %qr_hbm.1, bf16[1,256,512]{2,1,0:T(8,128)(2,1)} %cl_hbm.1, bf16[1,64,256]{2,1,0:T(8,128)(2,1)} %bitcast.1, bf16[1,32,512]{2,1,0:T(8,128)(2,1)} %nl_hbm.1, bf16[1,32,64]{2,1,0:T(8,128)(2,1)} %nr_hbm.1, ...), custom_call_target="tpu_custom_call" | custom-call | flops 7000000000 | bytes 7000000 | tf_op jit(solution)/shard_map/latent_attention/pallas_call | solution.py:313
  19.5 0.8 %copy.11 = bf16[1,128,2048]{2,1,0:T(8,128)(2,1)} copy(bf16[1,128,2048]{2,1,0:T(8,128)(2,1)S(1)} %latent_attention.1) | data formatting | bytes 1048576

commit v10 on v8

--- a/solution.py
+++ b/solution.py
@@ -252,12 +252,12 @@
             prepare_cached(1)
             turn(*CHUNKS[1])
         if index == 2 * PAIRS - 1:
+            onward(range(2))
+        if index == 2 * PAIRS:
+            onward(range(4, 5))
             pl.semaphore_wait(ready, 1)
             to_par[6].start()
             to_far.start()
-            onward(range(2))
-        if index == 2 * PAIRS:
-            onward(range(4, 5))
             prepare_cached(2)
             turn(*CHUNKS[2])
         if index == 3 * PAIRS:

time: 19.2 us -> 20 us (1.042)
  Pallas kernels: 17.7 us -> 18.5 us
    pallas_call x1, Pallas kernels: 17.7 us -> 18.5 us  [shards(): pl.pallas_call(kernel, out_shape=pltpu.VMEM((1, Q, HERE * DV), BF16), in_...]
where the time goes in v10:
time: 20 us; the launch traced here: 19.9 us
  Pallas kernels  18.5 us (92%)
  local copies, waits for them, and re-layouts  0.8 us (4%)
  between operations  0.66 us (3%)
    pallas_call x1, Pallas kernels, shards(): pl.pallas_call(kernel, out_shape=pltpu.VMEM((1, Q, HERE * DV), BF16), in_...  18.5 us
    unnamed x1, local copies, waits for them, and re-layouts  0.8 us

profile of v10, /device:TPU:1, one launch (start us, length us, event | category | flops | bytes accessed | tf_op | source)
XLA Modules:
  0.0 19.9 jit_solution(13959858227289300471)
XLA Ops:
  0.7 18.5 %latent_attention.1 = bf16[1,128,2048]{2,1,0:T(8,128)(2,1)S(1)} custom-call(bf16[1,128,8192]{2,1,0:T(8,128)(2,1)} %qn_hbm.1, bf16[1,128,4096]{2,1,0:T(8,128)(2,1)} %qr_hbm.1, bf16[1,256,512]{2,1,0:T(8,128)(2,1)} %cl_hbm.1, bf16[1,64,256]{2,1,0:T(8,128)(2,1)} %bitcast.1, bf16[1,32,512]{2,1,0:T(8,128)(2,1)} %nl_hbm.1, bf16[1,32,64]{2,1,0:T(8,128)(2,1)} %nr_hbm.1, ...), custom_call_target="tpu_custom_call" | custom-call | flops 7000000000 | bytes 7000000 | tf_op jit(solution)/shard_map/latent_attention/pallas_call | solution.py:312
  19.1 0.8 %copy.11 = bf16[1,128,2048]{2,1,0:T(8,128)(2,1)} copy(bf16[1,128,2048]{2,1,0:T(8,128)(2,1)S(1)} %latent_attention.1) | data formatting | bytes 1048576

commit v11 on v8

--- a/solution.py
+++ b/solution.py
@@ -73,7 +73,6 @@
         return pltpu.make_async_copy(src, dst, load_sem.at[index])
 
     loads = dict(
-        wk=local(0, wk_hbm, wk),
         qn=local(1, qn_hbm.at[0, :, pl.ds(pl.multiple_of(me * HERE * DH, HERE * DH), HERE * DH)], qn),
         qr=local(2, qr_hbm.at[0, :, pl.ds(pl.multiple_of(me * HERE * DR, HERE * DR), HERE * DR)], qr),
         cl=local(3, cl_hbm.at[0], lat.at[pl.ds(0, ROWS)]),
@@ -83,10 +82,14 @@
         ln=local(7, len_hbm, lens.at[0]),
         wv=local(8, wv_hbm, wv),
     )
+    part = HERE * DH // 4
+    for k in range(4):
+        columns = pl.ds(k * part, part)
+        loads[k] = local(9 + k, wk_hbm.at[:, columns], wk.at[:, columns])
     barrier = pltpu.get_barrier_semaphore()
     for peer in (sib, par):
         pl.semaphore_signal(barrier, inc=1, device_id={"ctx": peer}, device_id_type=MESH)
-    for name in ("wk", "qn", "qr", "cl", "cr", "nl", "nr", "ln"):
+    for name in ("qn", 0, 1, 2, 3, "qr", "cl", "cr", "nl", "nr", "ln"):
         loads[name].start()
     pl.semaphore_wait(barrier, 2)
     pl.semaphore_signal(ready, inc=1, device_id={"ctx": sib}, device_id_type=MESH)
@@ -129,17 +132,18 @@
     for pair in range(PAIRS):
         qt[pair, DC + DR :, :] = tail
 
-    loads["wk"].wait()
     loads["qn"].wait()
-    loads["qr"].wait()
     loads["wv"].start()
     for head in range(HERE):
+        if head % (HERE // 4) == 0:
+            loads[head // (HERE // 4)].wait()
         pair, side = head // 2, (head % 2) * Q
         part = lax.dot_general(
             wk[:, head * DH : (head + 1) * DH], qn[:, head * DH : (head + 1) * DH],
             (((1,), (1,)), ((), ())), preferred_element_type=F32,
         )
         qt[pair, :DC, side : side + Q] = part.astype(BF16)
+    loads["qr"].wait()
     for pair in range(PAIRS):
         turned = qr[:, pair * 2 * DR : (pair + 1) * 2 * DR].T
         qt[pair, DC : DC + DR, :Q] = turned[:DR]
@@ -335,7 +339,7 @@
             pltpu.VMEM((2 * ROWS, 2 * Q), BF16),
             pltpu.VMEM((1, 2 * Q), F32),
             pltpu.VMEM((1, 2 * Q), F32),
-            pltpu.SemaphoreType.DMA((9,)),
+            pltpu.SemaphoreType.DMA((13,)),
         ]
         + [pltpu.SemaphoreType.DMA((7,))] * 6
         + [pltpu.SemaphoreType.DMA((1,))] * 2

time: 19.2 us -> 19.3 us (level)
  no operation moved by 1% of the time
where the time goes in v11:
time: 19.3 us; the launch traced here: 19.2 us
  Pallas kernels  17.7 us (92%)
  local copies, waits for them, and re-layouts  0.8 us (4%)
  between operations  0.66 us (3%)
    pallas_call x1, Pallas kernels, shards(): pl.pallas_call(kernel, out_shape=pltpu.VMEM((1, Q, HERE * DV), BF16), in_...  17.7 us
    unnamed x1, local copies, waits for them, and re-layouts  0.8 us

profile of v11, /device:TPU:1, one launch (start us, length us, event | category | flops | bytes accessed | tf_op | source)
XLA Modules:
  0.0 19.2 jit_solution(16837966906742615019)
XLA Ops:
  0.7 17.7 %latent_attention.1 = bf16[1,128,2048]{2,1,0:T(8,128)(2,1)S(1)} custom-call(bf16[1,128,8192]{2,1,0:T(8,128)(2,1)} %qn_hbm.1, bf16[1,128,4096]{2,1,0:T(8,128)(2,1)} %qr_hbm.1, bf16[1,256,512]{2,1,0:T(8,128)(2,1)} %cl_hbm.1, bf16[1,64,256]{2,1,0:T(8,128)(2,1)} %bitcast.1, bf16[1,32,512]{2,1,0:T(8,128)(2,1)} %nl_hbm.1, bf16[1,32,64]{2,1,0:T(8,128)(2,1)} %nr_hbm.1, ...), custom_call_target="tpu_custom_call" | custom-call | flops 7000000000 | bytes 7000000 | tf_op jit(solution)/shard_map/latent_attention/pallas_call | solution.py:316
  18.4 0.8 %copy.11 = bf16[1,128,2048]{2,1,0:T(8,128)(2,1)} copy(bf16[1,128,2048]{2,1,0:T(8,128)(2,1)S(1)} %latent_attention.1) | data formatting | bytes 1048576
